TPU v7x, 256 devices: a whole 4x4x8 slice. The times are simulated.
256 devices in a mesh: row: 16 (over y_hi, z), col: 16 (over y_lo, x, core).
Axes of the slice: x: 4, y: 4 (y_hi: 2, y_lo: 2; y = y_hi * 2 + y_lo), z: 8, core: 2. Of those that a mesh axis runs over, the one named last changes fastest.
Arguments:
- obs_panel: bfloat16 [196608, 2048], P('row', 'col'), may hold values from -0.1875 to 0.1875
- skies: bfloat16 [196608, 256], P('row', 'col'), may hold values from -6 to 6
- panel_index: int32 [2048], replicated, may hold values from 0 to 196607
- prior_sum: float32 [196608, 256], P('row', 'col'), may hold values from -6 to 6
- apod: float32 [196608], P('row'), may hold values from 0.05 to 1
- proj_panel: bfloat16 [2048, 196608], P(None, ('row', 'col')), may hold values from -0.0546875 to 0.0546875
Outputs:
- reobserved: float32 [196608, 256], P('row', 'col')
- projection: float32 [2048, 256], P('row', 'col')
Inputs may be any that keep to these rules, and one draw needn't show every extreme that they name: `panel_index`: rows of the observed patch; a row may appear more than once.
All inputs are finite; a program needn't handle non-finite values.
Results may differ from a plain program's by a relative error of at most 0.0029.
Values may be sent and summed in bfloat16 or wider, within the bound.
No kernel may reach another device: no remote copies, remote signals or barrier semaphores. Data moves between devices by JAX's collectives and lax.ppermute only.
A program may use at most 64 MiB of HBM per device.

v0:
```python
import jax
import jax.numpy as jnp
from jax import lax
from jax.sharding import PartitionSpec as P


def on_device(obs_panel, skies, panel_index, prior_sum, apod, proj_panel):
    rows_blk = skies.shape[0]
    first_row = lax.axis_index("row") * rows_blk
    local_idx = panel_index - first_row
    inside = (local_idx >= 0) & (local_idx < rows_blk)
    taken = jnp.take(skies, jnp.clip(local_idx, 0, rows_blk - 1), axis=0)
    picked = jnp.where(inside[:, None], taken, jnp.zeros((), jnp.bfloat16))
    panel_maps = lax.psum(picked, "row").astype(jnp.float32).astype(jnp.bfloat16)
    panel_block = lax.all_to_all(panel_maps, "col", split_axis=0, concat_axis=1, tiled=True)
    partial_value = jnp.dot(obs_panel, panel_block, preferred_element_type=jnp.float32)
    summed = lax.psum_scatter(partial_value, "col", scatter_dimension=1, tiled=True)
    reobserved = prior_sum + summed
    weighted = (apod[:, None] * reobserved).astype(jnp.bfloat16)
    weighted_rows = lax.all_to_all(weighted, "col", split_axis=0, concat_axis=1, tiled=True)
    row_share = lax.psum_scatter(
        jnp.dot(proj_panel, weighted_rows, preferred_element_type=jnp.float32),
        "row",
        scatter_dimension=0,
        tiled=True,
    )
    projection = lax.psum_scatter(row_share, "col", scatter_dimension=1, tiled=True)
    return (reobserved, projection)


def solution(mesh):
    in_specs = (
        P("row", "col"),
        P("row", "col"),
        P(),
        P("row", "col"),
        P("row"),
        P(None, ("row", "col")),
    )
    out_specs = (P("row", "col"), P("row", "col"))
    return jax.shard_map(
        on_device, mesh=mesh, in_specs=in_specs, out_specs=out_specs, check_vma=False
    )
```

profile of v0, /device:TPU:32, one launch (start us, length us, event | category | flops | bytes accessed | tf_op | source)
XLA Modules:
  0.0 563.6 jit_solution(7166747702860846818)
XLA Ops:
  7.2 0.0 copy-start
  7.2 0.0 all-reduce.2.cloned.1.call-start
  7.2 0.9 compare_and_fusion.1
  8.1 0.7 fusion
  8.8 3.6 copy.9
  12.4 10.0 %gather_fusion = bf16[2048,16]{1,0:T(8,128)(2,1)} fusion(bf16[12288,16]{1,0:T(8,128)(2,1)} %copy.9, s32[2048]{0:T(1024)S(1)} %fusion), kind=kCustom, calls=%fused_computation | custom fusion | bytes 139264 | tf_op jit(solution)/shard_map/jit(_take)/gather | solution.py:12
  22.4 3.5 select_select_fusion
  26.0 1.8 copy.10
  27.8 0.0 all-reduce.2.cloned.1.call-update
  27.8 0.0 reduce-scatter.4.cloned.1.call-start
  27.9 143.0 %all-reduce.2.cloned.1.call-done = bf16[16,128,16]{1,2,0:T(8,128)(2,1)} async-done(((bf16[16,128,16]{1,2,0:T(8,128)(2,1)}), bf16[16,128,16]{1,2,0:T(8,128)(2,1)}) %all-reduce.2.cloned.1.call-update) | async-done | bytes 65552 | tf_op jit(solution)/shard_map/psum | solution.py:14
  170.8 11.2 %all_to_all.38 = bf16[16,128,16]{1,2,0:T(8,128)(2,1)S(1)} all-to-all(bf16[16,128,16]{1,2,0:T(8,128)(2,1)} %all-reduce.2.cloned.1.call-done), channel_id=1, replica_groups=mesh['row'=16,'col'=16] {'col'}, dimensions={0} | all-to-all | bytes 131072 | tf_op jit(solution)/shard_map/all_to_all | solution.py:15
  182.0 0.0 copy-done
  182.0 6.3 %convolution_bitcast_fusion = f32[12288,256]{0,1:T(8,128)} fusion(bf16[128,256]{0,1:T(8,128)(2,1)S(1)} %bitcast.23, bf16[12288,128]{1,0:T(8,128)(2,1)S(1)} %copy-done), kind=kOutput, calls=%fused_computation.1 | convolution fusion | flops 805306368 | bytes 15794176 | tf_op jit(solution)/shard_map/dot_general | solution.py:16
  188.4 0.0 copy-start.2
  188.4 0.0 reduce-scatter.4.cloned.1.call-update
  188.4 0.0 reduce-scatter.6.cloned.1.call-start
  188.5 81.3 %reduce-scatter.4.cloned.1.call-done = f32[12288,16]{0,1:T(8,128)} async-done(((f32[12288,256]{0,1:T(8,128)}), f32[12288,16]{0,1:T(8,128)}) %reduce-scatter.4.cloned.1.call-update) | async-done | bytes 786448 | tf_op jit(solution)/shard_map/reduce_scatter | solution.py:17
  269.7 0.0 copy-done.2
  269.7 0.0 copy-start.1
  269.7 2.5 multiply_convert_fusion
  272.3 11.9 %all_to_all.39 = bf16[16,768,16]{1,2,0:T(8,128)(2,1)S(1)} all-to-all(bf16[16,768,16]{1,2,0:T(8,128)(2,1)S(1)} %bitcast.20), channel_id=1, replica_groups=mesh['row'=16,'col'=16] {'col'}, dimensions={0} | all-to-all | bytes 786432 | tf_op jit(solution)/shard_map/all_to_all | solution.py:20
  284.2 0.0 copy-done.1
  284.2 2.4 convolution_bitcast_fusion.1
  286.6 0.0 reduce-scatter.6.cloned.1.call-update
  286.6 0.0 reduce-scatter.8.cloned.1.call-start
  286.6 206.0 %reduce-scatter.6.cloned.1.call-done = f32[128,256]{0,1:T(8,128)} async-done(((f32[2048,256]{0,1:T(8,128)}), f32[128,256]{0,1:T(8,128)}) %reduce-scatter.6.cloned.1.call-update) | async-done | bytes 131088 | tf_op jit(solution)/shard_map/reduce_scatter | solution.py:21
  492.6 0.0 reduce-scatter.8.cloned.1.call-update
  492.7 64.4 %reduce-scatter.8.cloned.1.call-done = f32[128,16]{0,1:T(8,128)} async-done(((f32[128,256]{0,1:T(8,128)}), f32[128,16]{0,1:T(8,128)}) %reduce-scatter.8.cloned.1.call-update) | async-done | bytes 8208 | tf_op jit(solution)/shard_map/reduce_scatter | solution.py:27
  (1 shorter events, 0.0 us)
Async XLA Ops:
  7.2 174.9 %copy-start = (bf16[12288,128]{1,0:T(8,128)(2,1)S(1)}, bf16[12288,128]{1,0:T(8,128)(2,1)}, u32[]{:S(2)}) copy-start(bf16[12288,128]{1,0:T(8,128)(2,1)} %param.6) | copy-start | bytes 9437188
  7.2 163.7 %all-reduce.2.cloned.1.call-start = ((), (), s32[]{:S(2)}) async-start(), calls=%async_computation.5 | async-start | bytes 131072 | tf_op jit(solution)/shard_map/psum | solution.py:14
  27.8 241.9 %reduce-scatter.4.cloned.1.call-start = ((), (), s32[]{:S(2)}) async-start(), calls=%async_computation.6 | async-start | bytes 13369344 | tf_op jit(solution)/shard_map/reduce_scatter | solution.py:17
  188.4 81.4 %copy-start.2 = (f32[12288]{0:T(1024)S(1)}, f32[12288]{0:T(1024)}, u32[]{:S(2)}) copy-start(f32[12288]{0:T(1024)} %param.10) | copy-start | bytes 147460
  188.4 304.2 %reduce-scatter.6.cloned.1.call-start = ((), (), s32[]{:S(2)}) async-start(), calls=%async_computation.7 | async-start | bytes 2228224 | tf_op jit(solution)/shard_map/reduce_scatter | solution.py:21
  269.7 14.5 %copy-start.1 = (bf16[2048,768]{1,0:T(8,128)(2,1)S(1)}, bf16[2048,768]{1,0:T(8,128)(2,1)}, u32[]{:S(2)}) copy-start(bf16[2048,768]{1,0:T(8,128)(2,1)} %param.11) | copy-start | bytes 9437188
  286.6 270.5 %reduce-scatter.8.cloned.1.call-start = ((), (), s32[]{:S(2)}) async-start(), calls=%async_computation.8 | async-start | bytes 139264 | tf_op jit(solution)/shard_map/reduce_scatter | solution.py:27
Sparse Core Ops, SparseCore 0:
  27.9 142.8 all-reduce.1
  188.5 81.1 reduce-scatter.3
  286.7 205.8 reduce-scatter.5
  495.7 61.3 reduce-scatter.7
where the time goes:
time: 564 us
  waiting for transfers between devices  495 us (88%)
  blocking collectives  23.1 us (4%)
  local copies, waits for them, and re-layouts  15.5 us (3%)
  between operations  13.8 us (2%)
  matrix products  8.7 us (2%)
  other arithmetic  7.61 us (1%)
    reduce_scatter x1, waiting for transfers between devices, on_device(): lax.psum_scatter(jnp.dot(proj_panel, weighted_rows, preferred_element_typ...  206 us
    psum x1, waiting for transfers between devices, on_device(): lax.psum(picked, 'row').astype(jnp.float32).astype(jnp.bfloat16)  143 us
    reduce_scatter x1, waiting for transfers between devices, on_device(): lax.psum_scatter(partial_value, 'col', scatter_dimension=1, tiled=True)  81.3 us
    reduce_scatter x1, waiting for transfers between devices, on_device(): lax.psum_scatter(row_share, 'col', scatter_dimension=1, tiled=True)  64.4 us
    all_to_all x1, blocking collectives, on_device(): lax.all_to_all(weighted, 'col', split_axis=0, concat_axis=1, tiled=True)  11.9 us
  transfers between devices with their start and end apart: 4, of which 4 were waited for; matrix products, arithmetic and copies ran while one was open for 0% of the time, Pallas kernels for 0%

commit v1 on v0

v1 whole, which is shorter than its diff:
```python
import jax
import jax.numpy as jnp
from jax import lax
from jax.experimental import pallas as pl
from jax.experimental.pallas import tpu as pltpu
from jax.sharding import PartitionSpec as P

F32, BF16 = jnp.float32, jnp.bfloat16
LANES = 128


def pick_kernel(first_ref, idx_ref, sky_ref, out_ref):
    evo, rows = sky_ref.shape
    groups = rows // LANES
    local = idx_ref[...] - first_ref[0]
    lane = lax.broadcasted_iota(jnp.int32, (LANES, local.shape[1]), 0)
    onehot = jnp.where(lane == (local & (LANES - 1)), 1.0, 0.0).astype(BF16)
    group = lax.shift_right_arithmetic(local, 7)
    total = jnp.zeros(out_ref.shape, F32)
    step = 16
    for start in range(0, groups, step):
        block = jnp.concatenate(
            [sky_ref[:, g * LANES : (g + 1) * LANES] for g in range(start, start + step)], axis=0
        )
        found = jnp.dot(block, onehot, preferred_element_type=F32)
        for g in range(step):
            total = total + jnp.where(group == start + g, found[g * evo : (g + 1) * evo], 0.0)
    out_ref[...] = total.astype(BF16)


def pick(first, idx, sky):
    evo, rows = sky.shape
    count = idx.shape[1]
    tile = 256
    return pl.pallas_call(
        pick_kernel,
        out_shape=jax.ShapeDtypeStruct((evo, count), BF16),
        grid_spec=pltpu.PrefetchScalarGridSpec(
            num_scalar_prefetch=1,
            grid=(count // tile,),
            in_specs=[
                pl.BlockSpec((1, tile), lambda i, _: (0, i)),
                pl.BlockSpec((evo, rows), lambda i, _: (0, 0)),
            ],
            out_specs=pl.BlockSpec((evo, tile), lambda i, _: (0, i)),
        ),
        cost_estimate=pl.CostEstimate(
            flops=2 * evo * rows * count, bytes_accessed=2 * evo * rows + 2 * evo * count, transcendentals=0
        ),
    )(first, idx, sky)


def gather(x, axis, n):
    return lax.all_to_all(jnp.broadcast_to(x[None], (n, *x.shape)), axis, 0, 0, tiled=True)


def on_device(n_row, n_col, obs, skies, idx, prior, apod, proj):
    rows_blk, evo = skies.shape
    sub = rows_blk // n_col
    count = idx.shape[0]
    first = (lax.axis_index("row") * rows_blk).astype(jnp.int32)
    picked = pick(first.reshape(1), idx.reshape(1, count), skies.T)
    shares = lax.all_to_all(picked.reshape(evo, n_row, count // n_row), "row", 1, 0, tiled=True)
    shares = shares.reshape(n_row, evo, count // n_row).astype(F32).sum(0).astype(BF16)
    mine = gather(shares, "row", n_row).transpose(1, 0, 2).reshape(evo, count)
    panel = gather(mine, "col", n_col).reshape(n_col * evo, count)

    obs_rows = lax.all_to_all(obs, "col", 0, 1, tiled=True)
    prior_t = prior.T
    prior_rows = lax.all_to_all(prior_t, "col", 1, 0, tiled=True)

    added = lax.dot_general(panel, obs_rows, (((1,), (1,)), ((), ())), preferred_element_type=F32)
    apod_sub = lax.dynamic_slice(apod, (lax.axis_index("col") * sub,), (sub,))
    reob = prior_rows + added
    weighted = (apod_sub[None, :] * reob).astype(BF16)
    partial = lax.dot_general(weighted, proj, (((1,), (1,)), ((), ())), preferred_element_type=F32)
    shared = lax.all_to_all(partial.astype(BF16).reshape(n_col, evo, -1), "col", 0, 0, tiled=True)
    column = shared.astype(F32).sum(0)
    column = lax.all_to_all(column.reshape(evo, n_row, -1), "row", 1, 0, tiled=True)
    projection = column.reshape(n_row, evo, -1).sum(0).T

    back = lax.all_to_all(added, "col", 0, 1, tiled=True)
    reobserved = (prior_t + back).T
    return reobserved, projection


def solution(mesh):
    n_row, n_col = mesh.shape["row"], mesh.shape["col"]

    def step(*args):
        return on_device(n_row, n_col, *args)

    return jax.shard_map(
        step,
        mesh=mesh,
        in_specs=(P("row", "col"), P("row", "col"), P(), P("row", "col"), P("row"), P(None, ("row", "col"))),
        out_specs=(P("row", "col"), P("row", "col")),
        check_vma=False,
    )
```

time: 564 us -> 190 us (0.34)
  waiting for transfers between devices: 495 us -> 93.9 us
  starting transfers between devices: 0.16 us -> 26.4 us
  blocking collectives: 23.1 us -> 38.2 us
  between operations: 13.8 us -> 0.71 us
  Pallas kernels: 0 us -> 6 us
    reduce_scatter x3 -> x0, waiting for transfers between devices: 352 us -> none  [the longest x1 206 us: on_device(): lax.psum_scatter(jnp.dot(proj_panel, weighted_rows, preferred_element_typ...]
    psum x1 -> x0, waiting for transfers between devices: 143 us -> none  [on_device(): lax.psum(picked, 'row').astype(jnp.float32).astype(jnp.bfloat16)]
    all_to_all x0 -> x6, waiting for transfers between devices: none -> 93.9 us  [the longest x1 42.2 us: on_device(): obs_rows = lax.all_to_all(obs, 'col', 0, 1, tiled=True)]
    all_to_all x0 -> x6, starting transfers between devices: none -> 26.4 us  [the longest x2 8.9 us: gather(): lax.all_to_all(jnp.broadcast_to(x[None], (n, *x.shape)), axis, 0, 0, tile...]
    all_to_all x2, blocking collectives: 23.1 us -> 38.2 us  [the longest x1 20.1 us: on_device(): lax.all_to_all(picked.reshape(evo, n_row, count // n_row), 'row', 1, 0, t...]
    gather x1 -> x0, local copies, waits for them, and re-layouts: 10 us -> none  [on_device(): taken = jnp.take(skies, jnp.clip(local_idx, 0, rows_blk - 1), axis=0)]
    all_to_all x2 -> x3, local copies, waits for them, and re-layouts: 1.86 us -> 8.81 us  [the longest x1 4.65 us: on_device(): obs_rows = lax.all_to_all(obs, 'col', 0, 1, tiled=True)]
    pallas_call x0 -> x1, Pallas kernels: none -> 6 us  [pick(): pl.pallas_call(pick_kernel, out_shape=jax.ShapeDtypeStruct((evo, count),...]
  transfers between devices with their start and end apart: 4 -> 6, of which waited for: 4 -> 6; matrix products, arithmetic and copies ran while one was open for 0% -> 7% of each run, Pallas kernels for 0% -> 0%
where the time goes in v1:
time: 190 us; the launch traced here: 189 us
  waiting for transfers between devices  93.9 us (49%)
  blocking collectives  38.2 us (20%)
  starting transfers between devices  26.4 us (14%)
  local copies, waits for them, and re-layouts  12.9 us (7%)
  matrix products  6.28 us (3%)
  Pallas kernels  6 us (3%)
  other arithmetic  4.35 us (2%)
    all_to_all x1, waiting for transfers between devices, on_device(): obs_rows = lax.all_to_all(obs, 'col', 0, 1, tiled=True)  42.2 us
    all_to_all x1, blocking collectives, on_device(): lax.all_to_all(picked.reshape(evo, n_row, count // n_row), 'row', 1, 0, t...  20.1 us
    all_to_all x2, waiting for transfers between devices, gather(): lax.all_to_all(jnp.broadcast_to(x[None], (n, *x.shape)), axis, 0, 0, tile...  18.2 us
    all_to_all x1, blocking collectives, on_device(): prior_rows = lax.all_to_all(prior_t, 'col', 1, 0, tiled=True)  18.1 us
    all_to_all x1, waiting for transfers between devices, on_device(): lax.all_to_all(partial.astype(BF16).reshape(n_col, evo, -1), 'col', 0, 0,...  14.4 us
    all_to_all x1, waiting for transfers between devices, on_device(): back = lax.all_to_all(added, 'col', 0, 1, tiled=True)  11.6 us
    all_to_all x2, starting transfers between devices, gather(): lax.all_to_all(jnp.broadcast_to(x[None], (n, *x.shape)), axis, 0, 0, tile...  8.9 us
    all_to_all x1, waiting for transfers between devices, on_device(): lax.all_to_all(column.reshape(evo, n_row, -1), 'row', 1, 0, tiled=True)  7.46 us
  transfers between devices with their start and end apart: 6, of which 6 were waited for; matrix products, arithmetic and copies ran while one was open for 7% of the time, Pallas kernels for 0%

profile of v1, /device:TPU:32, one launch (start us, length us, event | category | flops | bytes accessed | tf_op | source)
XLA Modules:
  0.0 188.7 jit_solution(1042439590883084970)
XLA Ops:
  0.6 0.0 copy-start
  0.7 6.0 %shard_map.77 = bf16[16,2048]{1,0:T(8,128)(2,1)} custom-call(s32[1]{0:T(128)} %bitcast.1.first_ref, s32[1,2048]{1,0:T(1,128)} %bitcast.60, bf16[16,12288]{1,0:T(8,128)(2,1)} %bitcast.59), custom_call_target="tpu_custom_call" | custom-call | flops 805306368 | bytes 458752 | tf_op jit(solution)/shard_map/pallas_call | solution.py:35
  6.6 0.9 copy_bitcast_fusion.3
  7.5 20.1 %all_to_all.90 = bf16[16,16,128]{2,0,1:T(8,128)(2,1)S(1)} all-to-all(bf16[16,16,128]{2,0,1:T(8,128)(2,1)S(1)} %copy_bitcast_fusion.3), channel_id=1, replica_groups=mesh['row'=16,'col'=16] {'row'}, dimensions={1} | all-to-all | bytes 131072 | tf_op jit(solution)/shard_map/all_to_all | solution.py:63
  27.7 0.6 broadcast_in_dim.6
  28.3 4.3 %all-to-all-start.1 = ((bf16[16,16,128]{2,1,0:T(8,128)(2,1)}), bf16[16,16,128]{2,1,0:T(8,128)(2,1)S(1)}, u32[]{:S(2)}, u32[]{:S(2)}) async-start(bf16[16,16,128]{2,1,0:T(8,128)(2,1)} %broadcast_in_dim.6), calls=%async_computation.1 | async-start | bytes 131072 | tf_op jit(solution)/shard_map/all_to_all | solution.py:54
  32.6 2.1 %copy.35 = f32[2,16,8,768]{3,2,0,1:T(8,128)} copy(f32[2,16,8,768]{3,2,1,0:T(8,128)} %bitcast.54) | data formatting | bytes 1572864 | tf_op jit(solution)/shard_map/all_to_all | solution.py:70
  34.7 7.1 %all-to-all-done.1 = bf16[16,16,128]{2,1,0:T(8,128)(2,1)S(1)} async-done(((bf16[16,16,128]{2,1,0:T(8,128)(2,1)}), bf16[16,16,128]{2,1,0:T(8,128)(2,1)S(1)}, u32[]{:S(2)}, u32[]{:S(2)}) %all-to-all-start.1) | async-done | bytes 65568 | tf_op jit(solution)/shard_map/all_to_all | solution.py:54
  41.7 18.1 %all_to_all.91 = f32[16,16,768]{2,0,1:T(8,128)} all-to-all(f32[16,16,768]{2,0,1:T(8,128)} %bitcast.53), channel_id=1, replica_groups=mesh['row'=16,'col'=16] {'col'}, dimensions={1} | all-to-all | bytes 1572864 | tf_op jit(solution)/shard_map/all_to_all | solution.py:70
  59.9 4.5 %all-to-all-start.3 = ((bf16[16,768,128]{2,1,0:T(8,128)(2,1)}), bf16[16,768,128]{2,1,0:T(8,128)(2,1)}, u32[]{:S(2)}, u32[]{:S(2)}) async-start(bf16[16,768,128]{2,1,0:T(8,128)(2,1)} %bitcast.52), calls=%async_computation.3 | async-start | bytes 6291456 | tf_op jit(solution)/shard_map/all_to_all | solution.py:68
  64.4 42.2 %all-to-all-done.3 = bf16[16,768,128]{2,1,0:T(8,128)(2,1)} async-done(((bf16[16,768,128]{2,1,0:T(8,128)(2,1)}), bf16[16,768,128]{2,1,0:T(8,128)(2,1)}, u32[]{:S(2)}, u32[]{:S(2)}) %all-to-all-start.3) | async-done | bytes 3145760 | tf_op jit(solution)/shard_map/all_to_all | solution.py:68
  106.6 1.1 broadcast_in_dim.16
  107.7 4.6 %all-to-all-start.2 = ((bf16[16,16,2048]{2,1,0:T(8,128)(2,1)}), bf16[16,16,2048]{2,1,0:T(8,128)(2,1)}, u32[]{:S(2)}, u32[]{:S(2)}) async-start(bf16[16,16,2048]{2,1,0:T(8,128)(2,1)} %broadcast_in_dim.16), calls=%async_computation.2 | async-start | bytes 2097152 | tf_op jit(solution)/shard_map/all_to_all | solution.py:54
  112.3 0.8 dynamic_slice.3
  113.1 4.7 %copy.22 = bf16[768,16,128]{0,2,1:T(8,128)(2,1)} copy(bf16[768,16,128]{2,0,1:T(8,128)(2,1)} %bitcast.7) | data formatting | bytes 6291456 | tf_op jit(solution)/shard_map/all_to_all | solution.py:68
  117.7 11.1 %all-to-all-done.2 = bf16[16,16,2048]{2,1,0:T(8,128)(2,1)} async-done(((bf16[16,16,2048]{2,1,0:T(8,128)(2,1)}), bf16[16,16,2048]{2,1,0:T(8,128)(2,1)}, u32[]{:S(2)}, u32[]{:S(2)}) %all-to-all-start.2) | async-done | bytes 1048608 | tf_op jit(solution)/shard_map/all_to_all | solution.py:54
  128.8 4.2 %fusion.1 = (bf16[256,768]{1,0:T(8,128)(2,1)S(1)}, f32[256,768]{1,0:T(8,128)}) fusion(f32[16,16,768]{2,0,1:T(8,128)} %all_to_all.91, f32[768]{0:T(1024)S(1)} %dynamic_slice.3, bf16[256,2048]{1,0:T(8,128)(2,1)} %bitcast.5, bf16[768,2048]{0,1:T(8,128)(2,1)} %bitcast.51), kind=kOutput, calls=%fused_computation.5 | convolution fusion | flops 805896192 | bytes 6163456 | tf_op jit(solution)/shard_map/dot_general | solution.py:72
  133.1 4.3 %all-to-all-start.4 = ((f32[16,16,768]{2,1,0:T(8,128)}), f32[16,16,768]{2,1,0:T(8,128)}, u32[]{:S(2)}, u32[]{:S(2)}) async-start(f32[16,16,768]{2,1,0:T(8,128)} %bitcast.56), calls=%async_computation.4 | async-start | bytes 1572864 | tf_op jit(solution)/shard_map/all_to_all | solution.py:82
  137.4 0.0 copy-done
  137.4 2.0 %convolution_convert_fusion = bf16[256,2048]{1,0:T(8,128)(2,1)} fusion(bf16[256,768]{1,0:T(8,128)(2,1)S(1)} %get-tuple-element.2, bf16[2048,768]{1,0:T(8,128)(2,1)S(1)} %copy-done), kind=kOutput, calls=%fused_computation | convolution fusion | flops 805830656 | bytes 4587520 | tf_op jit(solution)/shard_map/dot_general | solution.py:76
  139.4 11.6 %all-to-all-done.4 = f32[16,16,768]{2,1,0:T(8,128)} async-done(((f32[16,16,768]{2,1,0:T(8,128)}), f32[16,16,768]{2,1,0:T(8,128)}, u32[]{:S(2)}, u32[]{:S(2)}) %all-to-all-start.4) | async-done | bytes 786464 | tf_op jit(solution)/shard_map/all_to_all | solution.py:82
  151.0 4.3 %all-to-all-start.6 = ((bf16[16,16,2048]{2,1,0:T(8,128)(2,1)}), bf16[16,16,2048]{2,1,0:T(8,128)(2,1)}, u32[]{:S(2)}, u32[]{:S(2)}) async-start(bf16[16,16,2048]{2,1,0:T(8,128)(2,1)} %bitcast.57), calls=%async_computation.6 | async-start | bytes 2097152 | tf_op jit(solution)/shard_map/all_to_all | solution.py:77
  155.4 2.1 %copy.30 = f32[16,2,8,768]{3,2,0,1:T(8,128)} copy(f32[16,2,8,768]{3,2,1,0:T(8,128)} %bitcast.25) | data formatting | bytes 1572864 | tf_op jit(solution)/shard_map/all_to_all | solution.py:82
  157.5 14.4 %all-to-all-done.6 = bf16[16,16,2048]{2,1,0:T(8,128)(2,1)} async-done(((bf16[16,16,2048]{2,1,0:T(8,128)(2,1)}), bf16[16,16,2048]{2,1,0:T(8,128)(2,1)}, u32[]{:S(2)}, u32[]{:S(2)}) %all-to-all-start.6) | async-done | bytes 1048608 | tf_op jit(solution)/shard_map/all_to_all | solution.py:77
  171.9 1.4 convert_reduce_fusion
  173.3 0.7 copy_bitcast_fusion.1
  173.9 4.4 %all-to-all-start.7 = ((f32[16,16,128]{2,0,1:T(8,128)}), f32[16,16,128]{2,0,1:T(8,128)S(1)}, u32[]{:S(2)}, u32[]{:S(2)}) async-start(f32[16,16,128]{2,0,1:T(8,128)} %copy_bitcast_fusion.1), calls=%async_computation.7 | async-start | bytes 262144 | tf_op jit(solution)/shard_map/all_to_all | solution.py:79
  178.3 2.3 %fusion.2 = f32[12288,16]{0,1:T(8,128)} fusion(f32[16,12288]{1,0:T(8,128)} %bitcast.55, f32[12288,16]{0,1:T(8,128)} %param.9), kind=kLoop, calls=%fused_computation.7 | loop fusion | flops 196608 | bytes 2359296 | tf_op jit(solution)/shard_map/transpose | solution.py:83
  180.6 7.5 %all-to-all-done.7 = f32[16,16,128]{2,0,1:T(8,128)S(1)} async-done(((f32[16,16,128]{2,0,1:T(8,128)}), f32[16,16,128]{2,0,1:T(8,128)S(1)}, u32[]{:S(2)}, u32[]{:S(2)}) %all-to-all-start.7) | async-done | bytes 131104 | tf_op jit(solution)/shard_map/all_to_all | solution.py:79
  188.1 0.6 reduce_sum.32
  (2 shorter events, 0.0 us)
Async XLA Ops:
  0.6 136.7 %copy-start = (bf16[2048,768]{1,0:T(8,128)(2,1)S(1)}, bf16[2048,768]{1,0:T(8,128)(2,1)}, u32[]{:S(2)}) copy-start(bf16[2048,768]{1,0:T(8,128)(2,1)} %param.11) | copy-start | bytes 9437188
  28.3 13.5 %all-to-all-start.1 = ((bf16[16,16,128]{2,1,0:T(8,128)(2,1)}), bf16[16,16,128]{2,1,0:T(8,128)(2,1)S(1)}, u32[]{:S(2)}, u32[]{:S(2)}) async-start(bf16[16,16,128]{2,1,0:T(8,128)(2,1)} %broadcast_in_dim.6), calls=%async_computation.1 | async-start | bytes 131072 | tf_op jit(solution)/shard_map/all_to_all | solution.py:54
  59.9 46.7 %all-to-all-start.3 = ((bf16[16,768,128]{2,1,0:T(8,128)(2,1)}), bf16[16,768,128]{2,1,0:T(8,128)(2,1)}, u32[]{:S(2)}, u32[]{:S(2)}) async-start(bf16[16,768,128]{2,1,0:T(8,128)(2,1)} %bitcast.52), calls=%async_computation.3 | async-start | bytes 6291456 | tf_op jit(solution)/shard_map/all_to_all | solution.py:68
  107.7 21.1 %all-to-all-start.2 = ((bf16[16,16,2048]{2,1,0:T(8,128)(2,1)}), bf16[16,16,2048]{2,1,0:T(8,128)(2,1)}, u32[]{:S(2)}, u32[]{:S(2)}) async-start(bf16[16,16,2048]{2,1,0:T(8,128)(2,1)} %broadcast_in_dim.16), calls=%async_computation.2 | async-start | bytes 2097152 | tf_op jit(solution)/shard_map/all_to_all | solution.py:54
  133.1 18.0 %all-to-all-start.4 = ((f32[16,16,768]{2,1,0:T(8,128)}), f32[16,16,768]{2,1,0:T(8,128)}, u32[]{:S(2)}, u32[]{:S(2)}) async-start(f32[16,16,768]{2,1,0:T(8,128)} %bitcast.56), calls=%async_computation.4 | async-start | bytes 1572864 | tf_op jit(solution)/shard_map/all_to_all | solution.py:82
  151.0 20.8 %all-to-all-start.6 = ((bf16[16,16,2048]{2,1,0:T(8,128)(2,1)}), bf16[16,16,2048]{2,1,0:T(8,128)(2,1)}, u32[]{:S(2)}, u32[]{:S(2)}) async-start(bf16[16,16,2048]{2,1,0:T(8,128)(2,1)} %bitcast.57), calls=%async_computation.6 | async-start | bytes 2097152 | tf_op jit(solution)/shard_map/all_to_all | solution.py:77
  173.9 14.1 %all-to-all-start.7 = ((f32[16,16,128]{2,0,1:T(8,128)}), f32[16,16,128]{2,0,1:T(8,128)S(1)}, u32[]{:S(2)}, u32[]{:S(2)}) async-start(f32[16,16,128]{2,0,1:T(8,128)} %copy_bitcast_fusion.1), calls=%async_computation.7 | async-start | bytes 262144 | tf_op jit(solution)/shard_map/all_to_all | solution.py:79

commit v2 on v1

v2 whole, which is shorter than its diff:
```python
import functools

import jax
import jax.numpy as jnp
from jax import lax
from jax.experimental import pallas as pl
from jax.experimental.pallas import tpu as pltpu
from jax.sharding import PartitionSpec as P

F32, BF16 = jnp.float32, jnp.bfloat16
LANES = 128
WIDE = 256
MIB = 1 << 20
NT = (((1,), (1,)), ((), ()))


def whole(n):
    return [pl.BlockSpec(memory_space=pltpu.VMEM)] * n


def cost(flops, nbytes):
    return pl.CostEstimate(flops=flops, bytes_accessed=nbytes, transcendentals=0)


def pack_kernel(dests, obs_ref, prior_ref, out_ref):
    sub = obs_ref.shape[0] // dests
    evo = prior_ref.shape[0]
    for d in range(dests):
        out_ref[d, :sub] = obs_ref[d * sub : (d + 1) * sub]
        for l in range(sub // LANES):
            at = d * sub + l * LANES
            value = prior_ref[:, at : at + LANES]
            high = value.astype(BF16)
            row = sub + l * 2 * evo
            out_ref[d, row : row + evo] = high
            out_ref[d, row + evo : row + 2 * evo] = (value - high.astype(F32)).astype(BF16)


def pack(obs, prior_t, n_col):
    rows, width = obs.shape
    evo = prior_t.shape[0]
    sub = rows // n_col
    depth = sub + 2 * evo * sub // LANES
    dests = 4
    return pl.pallas_call(
        functools.partial(pack_kernel, dests),
        out_shape=jax.ShapeDtypeStruct((n_col, depth, width), BF16),
        grid=(n_col // dests,),
        in_specs=[
            pl.BlockSpec((dests * sub, width), lambda i: (i, 0)),
            pl.BlockSpec((evo, dests * sub), lambda i: (0, i)),
        ],
        out_specs=pl.BlockSpec((dests, depth, width), lambda i: (i, 0, 0)),
        cost_estimate=cost(0, 2 * 2 * n_col * depth * width),
    )(obs, prior_t)


def pick_kernel(first_ref, idx_ref, sky_ref, out_ref):
    evo, rows = sky_ref.shape
    groups = rows // WIDE
    local = idx_ref[...] - first_ref[0]
    place = lax.broadcasted_iota(jnp.int32, (WIDE, local.shape[1]), 0)
    onehot = jnp.where(place == (local & (WIDE - 1)), 1.0, 0.0).astype(BF16)
    group = lax.shift_right_arithmetic(local, WIDE.bit_length() - 1)
    total = jnp.zeros(out_ref.shape, F32)
    step = 16
    for start in range(0, groups, step):
        block = jnp.concatenate(
            [sky_ref[:, g * WIDE : (g + 1) * WIDE] for g in range(start, start + step)], axis=0
        )
        found = jnp.dot(block, onehot, preferred_element_type=F32)
        for g in range(step):
            total = total + jnp.where(group == start + g, found[g * evo : (g + 1) * evo], 0.0)
    out_ref[...] = total.astype(BF16)


def pick(first, idx, sky):
    evo, rows = sky.shape
    count = idx.shape[1]
    tile = 512
    return pl.pallas_call(
        pick_kernel,
        out_shape=jax.ShapeDtypeStruct((evo, count), BF16),
        grid_spec=pltpu.PrefetchScalarGridSpec(
            num_scalar_prefetch=1,
            grid=(count // tile,),
            in_specs=[
                pl.BlockSpec((1, tile), lambda i, _: (0, i)),
                pl.BlockSpec((evo, rows), lambda i, _: (0, 0)),
            ],
            out_specs=pl.BlockSpec((evo, tile), lambda i, _: (0, i)),
        ),
        cost_estimate=cost(2 * evo * rows * count, 2 * evo * rows + 2 * evo * count),
    )(first, idx, sky)


def main_kernel(
    me_ref, msg_ref, own_ref, other_ref, apod_ref, proj_ref, p_own, p_other, s_own, s_other, panel, weighted
):
    chips, evo, count = own_ref.shape
    prows, sub = proj_ref.shape
    me = me_ref[0]
    core = me % 2
    half = chips * evo
    for m in range(chips):
        panel[m * evo : (m + 1) * evo] = own_ref[m]
        panel[half + m * evo : half + (m + 1) * evo] = other_ref[m]
    sources = [2 * m + jnp.bitwise_xor(core, b) for b in range(2) for m in range(chips)]
    for n in range(sub // WIDE):
        rows = slice(n * WIDE, (n + 1) * WIDE)
        added = jnp.zeros((2 * half, WIDE), F32)
        for k in range(chips):
            obs = jnp.concatenate([msg_ref[2 * k, rows], msg_ref[2 * k + 1, rows]], axis=1)
            added += lax.dot_general(
                panel[:, k * WIDE : (k + 1) * WIDE], obs, NT, preferred_element_type=F32
            )
        s_own[:, :, rows] = added[:half].astype(BF16).reshape(chips, evo, WIDE)
        s_other[:, :, rows] = added[half:].astype(BF16).reshape(chips, evo, WIDE)
        for l in range(WIDE // LANES):
            block = n * (WIDE // LANES) + l
            row = sub + block * 2 * evo
            prior = jnp.concatenate(
                [
                    msg_ref[s, row : row + evo].astype(F32) + msg_ref[s, row + evo : row + 2 * evo].astype(F32)
                    for s in sources
                ],
                axis=0,
            )
            weight = apod_ref[pl.ds(me * (sub // LANES) + block, 1), :]
            value = weight * (prior + added[:, l * LANES : (l + 1) * LANES])
            weighted[:, block * LANES : (block + 1) * LANES] = value.astype(BF16)
    for n in range(prows // WIDE):
        cols = slice(n * WIDE, (n + 1) * WIDE)
        part = lax.dot_general(weighted[...], proj_ref[cols], NT, preferred_element_type=F32)
        p_own[:, :, cols] = part[:half].reshape(chips, evo, WIDE)
        p_other[:, :, cols] = part[half:].reshape(chips, evo, WIDE)


def main_step(me, msg, own, other, apod, proj):
    chips, evo, count = own.shape
    prows, sub = proj.shape
    total = 2 * chips * evo
    return pl.pallas_call(
        main_kernel,
        out_shape=(
            jax.ShapeDtypeStruct((chips, evo, prows), F32),
            jax.ShapeDtypeStruct((chips, evo, prows), F32),
            jax.ShapeDtypeStruct((chips, evo, sub), BF16),
            jax.ShapeDtypeStruct((chips, evo, sub), BF16),
        ),
        in_specs=[pl.BlockSpec(memory_space=pltpu.SMEM)] + whole(5),
        out_specs=tuple(whole(4)),
        scratch_shapes=[pltpu.VMEM((total, count), BF16), pltpu.VMEM((total, sub), BF16)],
        compiler_params=pltpu.CompilerParams(vmem_limit_bytes=28 * MIB),
        cost_estimate=cost(2 * total * sub * (count + prows), 2 * msg.size + 2 * proj.size + 4 * total * prows),
    )(me, msg, own, other, apod, proj)


def home_kernel(p_own, p_got, s_own, s_got, out_ref):
    prows, sub = p_own.shape[2], s_own.shape[2]
    out_ref[:, :, :prows] = (p_own[...] + p_got[...]).astype(BF16)
    out_ref[:, :, prows : prows + sub] = s_own[...]
    out_ref[:, :, prows + sub :] = s_got[...]


def sum_kernel(msg_ref, out_ref):
    width = out_ref.shape[2]
    for n in range(out_ref.shape[0]):
        out_ref[n] = jnp.sum(msg_ref[:, :, n * width : (n + 1) * width].astype(F32), axis=0)


def add_kernel(prows, core_ref, msg_ref, prior_ref, out_ref):
    chips = msg_ref.shape[0]
    sub = prior_ref.shape[1] // (2 * chips)
    core = core_ref[0]
    for m in range(chips):
        for b in range(2):
            at = pl.ds(pl.multiple_of((2 * m + jnp.bitwise_xor(core, b)) * sub, LANES), sub)
            came = msg_ref[m, :, prows + b * sub : prows + (b + 1) * sub].astype(F32)
            out_ref[:, at] = prior_ref[:, at] + came


EARLY, LATE = (3, 5, 6, 7, 2), (1, 4)


def stack_kernel(*refs):
    for n, ref in enumerate(refs[:-1]):
        refs[-1][n] = ref[...]


def stack(parts):
    return pl.pallas_call(
        stack_kernel,
        out_shape=jax.ShapeDtypeStruct((len(parts), *parts[0].shape), parts[0].dtype),
        in_specs=whole(len(parts)),
        out_specs=whole(1)[0],
        cost_estimate=cost(0, 4 * len(parts) * parts[0].size),
    )(*parts)


def swap(x, axis, bits, n):
    return lax.ppermute(x, axis, [(i, i ^ bits) for i in range(n)])


def on_device(n_row, n_col, obs, skies, idx, prior, apod, proj):
    rows_blk, evo = skies.shape
    sub = rows_blk // n_col
    count = idx.shape[0]
    prows = proj.shape[0]
    chips = n_col // 2
    prior_t = prior.T
    me = lax.axis_index("col").astype(jnp.int32)
    first = (lax.axis_index("row") * rows_blk).astype(jnp.int32)
    picked = pick(first.reshape(1), idx.reshape(1, count), skies.T)
    far = swap(picked, "row", n_row // 2, n_row)
    packed, far = lax.optimization_barrier((pack(obs, prior_t, n_col), far))
    msg = lax.all_to_all(packed, "col", 0, 0, tiled=True)
    picked = picked + far
    for group in ((1, 2, 3), (4,)):
        parts = [swap(picked, "row", k, n_row) for k in group]
        for part in parts:
            picked = picked + part
    copies = jnp.broadcast_to(picked[None], (chips, evo, count))
    msg, copies = lax.optimization_barrier((msg, copies))
    same = [[2 * m + b for m in range(chips)] for b in range(2)]
    own = lax.all_to_all(copies, "col", 0, 0, tiled=True, axis_index_groups=same)
    other = swap(own, "col", 1, n_col)

    p_own, p_other, s_own, s_other = main_step(
        me.reshape(1), msg, own, other, apod.reshape(rows_blk // LANES, LANES), proj
    )
    p_got = swap(p_other, "col", 1, n_col)
    s_got = swap(s_other, "col", 1, n_col)
    home = pl.pallas_call(
        home_kernel,
        out_shape=jax.ShapeDtypeStruct((chips, evo, prows + 2 * sub), BF16),
        in_specs=whole(4),
        out_specs=whole(1)[0],
        compiler_params=pltpu.CompilerParams(vmem_limit_bytes=16 * MIB),
        cost_estimate=cost(p_own.size, 10 * p_own.size),
    )(p_own, p_got, s_own, s_got)
    same = [[2 * m + b for m in range(chips)] for b in range(2)]
    home = lax.all_to_all(home, "col", 0, 0, tiled=True, axis_index_groups=same)
    share = pl.pallas_call(
        sum_kernel,
        out_shape=jax.ShapeDtypeStruct((n_row, evo, prows // n_row), F32),
        in_specs=whole(1),
        out_specs=whole(1)[0],
        cost_estimate=cost(home.size, 2 * home.size),
    )(home)
    share = lax.all_to_all(share, "row", 0, 0, tiled=True)
    projection = share.sum(0).T
    reobserved = pl.pallas_call(
        functools.partial(add_kernel, prows),
        out_shape=jax.ShapeDtypeStruct((evo, rows_blk), F32),
        in_specs=[pl.BlockSpec(memory_space=pltpu.SMEM)] + whole(2),
        out_specs=whole(1)[0],
        cost_estimate=cost(prior.size, 10 * prior.size),
    )((me % 2).reshape(1), home, prior_t).T
    return reobserved, projection


def solution(mesh):
    n_row, n_col = mesh.shape["row"], mesh.shape["col"]
    return jax.shard_map(
        functools.partial(on_device, n_row, n_col),
        mesh=mesh,
        in_specs=(P("row", "col"), P("row", "col"), P(), P("row", "col"), P("row"), P(None, ("row", "col"))),
        out_specs=(P("row", "col"), P("row", "col")),
        check_vma=False,
    )
```

time: 190 us -> 135 us (0.71)
  waiting for transfers between devices: 93.9 us -> 55.3 us
  local copies, waits for them, and re-layouts: 12.9 us -> 0.05 us
  Pallas kernels: 6 us -> 17.1 us
  matrix products: 6.28 us -> 0 us
  blocking collectives: 38.2 us -> 32.3 us
  other arithmetic: 4.35 us -> 0.67 us
    all_to_all x6 -> x2, waiting for transfers between devices: 93.9 us -> 40.3 us  [the longest x1 33.2 us: on_device(): msg = lax.all_to_all(packed, 'col', 0, 0, tiled=True)]
    ppermute x0 -> x8, waiting for transfers between devices: none -> 15 us  [swap(): return lax.ppermute(x, axis, [(i, i ^ bits) for i in range(n)])]
    pallas_call x0 -> x5, Pallas kernels: none -> 13.4 us  [the longest x1 4.56 us: main_step(): pl.pallas_call(main_kernel, out_shape=(jax.ShapeDtypeStruct((chips, evo,...]
    ppermute x0 -> x8, starting transfers between devices: none -> 13.2 us  [swap(): return lax.ppermute(x, axis, [(i, i ^ bits) for i in range(n)])]
    all_to_all x6 -> x2, starting transfers between devices: 26.4 us -> 14.8 us  [the longest x1 9.94 us: on_device(): share = lax.all_to_all(share, 'row', 0, 0, tiled=True)]
    all_to_all x3 -> x0, local copies, waits for them, and re-layouts: 8.81 us -> none  [the longest x1 4.65 us: on_device(): obs_rows = lax.all_to_all(obs, 'col', 0, 1, tiled=True)]
    dot_general x2 -> x0, matrix products: 6.28 us -> none  [the longest x1 4.25 us: on_device(): lax.dot_general(panel, obs_rows, (((1,), (1,)), ((), ())), preferred_elem...]
    all_to_all x2, blocking collectives: 38.2 us -> 32.3 us  [the longest x1 18 us: on_device(): home = lax.all_to_all(home, 'col', 0, 0, tiled=True, axis_index_groups=same)]
  transfers between devices with their start and end apart: 6 -> 10, of which waited for: 6 -> 7; matrix products, arithmetic and copies ran while one was open for 7% -> 0% of each run, Pallas kernels for 0% -> 5%
where the time goes in v2:
time: 135 us; the launch traced here: 134 us
  waiting for transfers between devices  55.3 us (41%)
  blocking collectives  32.3 us (24%)
  starting transfers between devices  28 us (21%)
  Pallas kernels  17.1 us (13%)
    all_to_all x1, waiting for transfers between devices, on_device(): msg = lax.all_to_all(packed, 'col', 0, 0, tiled=True)  33.2 us
    all_to_all x1, blocking collectives, on_device(): home = lax.all_to_all(home, 'col', 0, 0, tiled=True, axis_index_groups=same)  18 us
    ppermute x8, waiting for transfers between devices, swap(): return lax.ppermute(x, axis, [(i, i ^ bits) for i in range(n)])  15 us
    all_to_all x1, blocking collectives, on_device(): lax.all_to_all(copies, 'col', 0, 0, tiled=True, axis_index_groups=same)  14.3 us
    ppermute x8, starting transfers between devices, swap(): return lax.ppermute(x, axis, [(i, i ^ bits) for i in range(n)])  13.2 us
    all_to_all x1, starting transfers between devices, on_device(): share = lax.all_to_all(share, 'row', 0, 0, tiled=True)  9.94 us
    all_to_all x1, waiting for transfers between devices, on_device(): share = lax.all_to_all(share, 'row', 0, 0, tiled=True)  7.1 us
    all_to_all x1, starting transfers between devices, on_device(): msg = lax.all_to_all(packed, 'col', 0, 0, tiled=True)  4.84 us
  transfers between devices with their start and end apart: 10, of which 7 were waited for; matrix products, arithmetic and copies ran while one was open for 0% of the time, Pallas kernels for 5%

profile of v2, /device:TPU:32, one launch (start us, length us, event | category | flops | bytes accessed | tf_op | source)
XLA Modules:
  0.0 134.1 jit_solution(748194387053696234)
XLA Ops:
  0.6 3.7 %shard_map.78 = bf16[16,2048]{1,0:T(8,128)(2,1)} custom-call(s32[1]{0:T(128)} %bitcast.3.first_ref, s32[1,2048]{1,0:T(1,128)} %bitcast.15, bf16[16,12288]{1,0:T(8,128)(2,1)} %bitcast.14), custom_call_target="tpu_custom_call" | custom-call | flops 805306368 | bytes 458752 | tf_op jit(solution)/shard_map/pallas_call | solution.py:81
  4.3 3.2 %collective-permute-start = (bf16[16,2048]{1,0:T(8,128)(2,1)}, bf16[16,2048]{1,0:T(8,128)(2,1)S(1)}, u32[]{:S(2)}, u32[]{:S(2)}) collective-permute-start(bf16[16,2048]{1,0:T(8,128)(2,1)} %shard_map.78), channel_id=1, source_target_pairs={{0,128},{16,144},{32,160},{48,176},{64,192},{80,208},{96,224},{112... | collective-permute-start | bytes 196616 | tf_op jit(solution)/shard_map/ppermute | solution.py:202
  7.5 4.5 %shard_map.77 = bf16[16,960,128]{2,1,0:T(8,128)(2,1)} custom-call(bf16[12288,128]{1,0:T(8,128)(2,1)} %obs_ref.1, f32[16,12288]{1,0:T(8,128)} %bitcast.10), custom_call_target="tpu_custom_call" | custom-call | bytes 7864320 | tf_op jit(solution)/shard_map/pallas_call | solution.py:45
  12.0 0.0 collective-permute-done
  12.0 4.8 %all-to-all-start = ((bf16[16,960,128]{2,1,0:T(8,128)(2,1)}), bf16[16,960,128]{2,1,0:T(8,128)(2,1)}, u32[]{:S(2)}, u32[]{:S(2)}) async-start(bf16[16,960,128]{2,1,0:T(8,128)(2,1)} %shard_map.77), calls=%async_computation | async-start | bytes 7864320 | tf_op jit(solution)/shard_map/all_to_all | solution.py:217
  16.9 0.0 copy-done.2
  16.9 2.0 %collective-permute-start.3 = (bf16[16,2048]{1,0:T(8,128)(2,1)S(1)}, bf16[16,2048]{1,0:T(8,128)(2,1)S(1)}, u32[]{:S(2)}, u32[]{:S(2)}) collective-permute-start(bf16[16,2048]{1,0:T(8,128)(2,1)S(1)} %add.20), channel_id=1, source_target_pairs={{0,48},{16,32},{32,16},{48,0},{64,112},{80,96},{96,80},{112,64},{1... | collective-permute-start | bytes 196616 | tf_op jit(solution)/shard_map/ppermute | solution.py:202
  18.9 1.5 %collective-permute-start.2 = (bf16[16,2048]{1,0:T(8,128)(2,1)S(1)}, bf16[16,2048]{1,0:T(8,128)(2,1)S(1)}, u32[]{:S(2)}, u32[]{:S(2)}) collective-permute-start(bf16[16,2048]{1,0:T(8,128)(2,1)S(1)} %add.20), channel_id=1, source_target_pairs={{0,32},{16,48},{32,0},{48,16},{64,96},{80,112},{96,64},{112,80},{1... | collective-permute-start | bytes 196616 | tf_op jit(solution)/shard_map/ppermute | solution.py:202
  20.4 1.4 %collective-permute-start.1 = (bf16[16,2048]{1,0:T(8,128)(2,1)S(1)}, bf16[16,2048]{1,0:T(8,128)(2,1)S(1)}, u32[]{:S(2)}, u32[]{:S(2)}) collective-permute-start(bf16[16,2048]{1,0:T(8,128)(2,1)S(1)} %add.20), channel_id=1, source_target_pairs={{0,16},{16,0},{32,48},{48,32},{64,80},{80,64},{96,112},{112,96},{1... | collective-permute-start | bytes 196616 | tf_op jit(solution)/shard_map/ppermute | solution.py:202
  21.8 0.0 collective-permute-done.3
  21.8 3.1 %collective-permute-done.2 = bf16[16,2048]{1,0:T(8,128)(2,1)S(1)} collective-permute-done((bf16[16,2048]{1,0:T(8,128)(2,1)S(1)}, bf16[16,2048]{1,0:T(8,128)(2,1)S(1)}, u32[]{:S(2)}, u32[]{:S(2)}) %collective-permute-start.2) | collective-permute-done | bytes 65568 | tf_op jit(solution)/shard_map/ppermute | solution.py:202
  24.9 2.0 %collective-permute-done.1 = bf16[16,2048]{1,0:T(8,128)(2,1)S(1)} collective-permute-done((bf16[16,2048]{1,0:T(8,128)(2,1)S(1)}, bf16[16,2048]{1,0:T(8,128)(2,1)S(1)}, u32[]{:S(2)}, u32[]{:S(2)}) %collective-permute-start.1) | collective-permute-done | bytes 65568 | tf_op jit(solution)/shard_map/ppermute | solution.py:202
  27.0 4.6 %collective-permute-start.4 = (bf16[16,2048]{1,0:T(8,128)(2,1)S(1)}, bf16[16,2048]{1,0:T(8,128)(2,1)S(1)}, u32[]{:S(2)}, u32[]{:S(2)}) collective-permute-start(bf16[16,2048]{1,0:T(8,128)(2,1)S(1)} %add_add_fusion), channel_id=1, source_target_pairs={{0,64},{16,80},{32,96},{48,112},{64,0},{80,16},{96,32},{112,48},{1... | collective-permute-start | bytes 196616 | tf_op jit(solution)/shard_map/ppermute | solution.py:202
  31.5 5.1 %collective-permute-done.4 = bf16[16,2048]{1,0:T(8,128)(2,1)S(1)} collective-permute-done((bf16[16,2048]{1,0:T(8,128)(2,1)S(1)}, bf16[16,2048]{1,0:T(8,128)(2,1)S(1)}, u32[]{:S(2)}, u32[]{:S(2)}) %collective-permute-start.4) | collective-permute-done | bytes 65568 | tf_op jit(solution)/shard_map/ppermute | solution.py:202
  36.7 33.2 %all-to-all-done.msg_ref = bf16[16,960,128]{2,1,0:T(8,128)(2,1)} async-done(((bf16[16,960,128]{2,1,0:T(8,128)(2,1)}), bf16[16,960,128]{2,1,0:T(8,128)(2,1)}, u32[]{:S(2)}, u32[]{:S(2)}) %all-to-all-start) | async-done | bytes 3932192 | tf_op jit(solution)/shard_map/all_to_all | solution.py:217
  69.9 14.3 %all_to_all.20.own_ref = bf16[8,16,2048]{2,1,0:T(8,128)(2,1)} all-to-all(bf16[8,16,2048]{2,1,0:T(8,128)(2,1)S(1)} %broadcast_in_dim.2), channel_id=1, replica_groups={{0,2,4,6,8,10,12,14},{1,3,5,7,9,11,13,15},{16,18,20,22,24,26,28,30},{17..., dimensions={0} | all-to-all | bytes 1048576 | tf_op jit(solution)/shard_map/all_to_all | solution.py:226
  84.2 0.0 collective-permute-start.5
  84.2 2.2 %collective-permute-done.5.other_ref = bf16[8,16,2048]{2,1,0:T(8,128)(2,1)} collective-permute-done((bf16[8,16,2048]{2,1,0:T(8,128)(2,1)}, bf16[8,16,2048]{2,1,0:T(8,128)(2,1)}, u32[]{:S(2)}, u32[]{:S(2)}) %collective-permute-start.5) | collective-permute-done | bytes 524320 | tf_op jit(solution)/shard_map/ppermute | solution.py:202
  86.5 0.0 copy-done
  86.5 0.0 copy-done.1
  86.5 4.6 %shard_map.79 = (f32[8,16,2048]{2,1,0:T(8,128)S(1)}, f32[8,16,2048]{2,1,0:T(8,128)S(1)}, bf16[8,16,768]{2,1,0:T(8,128)(2,1)S(1)}, bf16[8,16,768]{2,1,0:T(8,128)(2,1)S(1)}) custom-call(s32[1]{0:T(128)} %bitcast.1.me_ref, bf16[16,960,128]{2,1,0:T(8,128)(2,1)} %all-to-all-done.msg_ref, bf16[8,16,2048]{2,1,0:T(8,128)(2,1)} %all_to_all.20.own_ref, ...), custom_call_target="tpu_custom_call" | custom-call | flops 1610612736 | bytes 9175040 | tf_op jit(solution)/shard_map/pallas_call | solution.py:143
  91.1 0.2 collective-permute-start.6
  91.3 0.4 collective-permute-start.7
  91.7 2.4 %collective-permute-done.7.s_got = bf16[8,16,768]{2,1,0:T(8,128)(2,1)S(1)} collective-permute-done((bf16[8,16,768]{2,1,0:T(8,128)(2,1)S(1)}, bf16[8,16,768]{2,1,0:T(8,128)(2,1)S(1)}, u32[]{:S(2)}, u32[]{:S(2)}) %collective-permute-start.7) | collective-permute-done | bytes 196640 | tf_op jit(solution)/shard_map/ppermute | solution.py:202
  94.1 0.0 collective-permute-done.6.p_got
  94.1 0.1 shard_map.80
  94.2 18.0 %all_to_all.21.msg_ref = bf16[8,16,3584]{2,1,0:T(8,128)(2,1)} all-to-all(bf16[8,16,3584]{2,1,0:T(8,128)(2,1)S(1)} %shard_map.80), channel_id=1, replica_groups={{0,2,4,6,8,10,12,14},{1,3,5,7,9,11,13,15},{16,18,20,22,24,26,28,30},{17..., dimensions={0} | all-to-all | bytes 1835008 | tf_op jit(solution)/shard_map/all_to_all | solution.py:243
  112.2 1.9 %shard_map.82 = f32[16,16,128]{2,1,0:T(8,128)} custom-call(bf16[8,16,3584]{2,1,0:T(8,128)(2,1)} %all_to_all.21.msg_ref), custom_call_target="tpu_custom_call" | custom-call | flops 458752 | bytes 917504 | tf_op jit(solution)/shard_map/pallas_call | solution.py:244
  114.1 9.9 %all-to-all-start.3 = ((f32[16,16,128]{2,1,0:T(8,128)}), f32[16,16,128]{2,1,0:T(8,128)S(1)}, u32[]{:S(2)}, u32[]{:S(2)}) async-start(f32[16,16,128]{2,1,0:T(8,128)} %shard_map.82), calls=%async_computation.3 | async-start | bytes 262144 | tf_op jit(solution)/shard_map/all_to_all | solution.py:251
  124.0 2.4 %shard_map.81 = f32[16,12288]{1,0:T(8,128)} custom-call(s32[1]{0:T(128)} %bitcast.core_ref, bf16[8,16,3584]{2,1,0:T(8,128)(2,1)} %all_to_all.21.msg_ref, f32[16,12288]{1,0:T(8,128)} %bitcast.11), custom_call_target="tpu_custom_call" | custom-call | flops 196608 | bytes 1966080 | tf_op jit(solution)/shard_map/pallas_call | solution.py:253
  126.4 7.1 %all-to-all-done.3 = f32[16,16,128]{2,1,0:T(8,128)S(1)} async-done(((f32[16,16,128]{2,1,0:T(8,128)}), f32[16,16,128]{2,1,0:T(8,128)S(1)}, u32[]{:S(2)}, u32[]{:S(2)}) %all-to-all-start.3) | async-done | bytes 131104 | tf_op jit(solution)/shard_map/all_to_all | solution.py:251
  133.5 0.6 reduce_sum.9
  (7 shorter events, 0.1 us)
Async XLA Ops:
  4.3 7.7 %collective-permute-start = (bf16[16,2048]{1,0:T(8,128)(2,1)}, bf16[16,2048]{1,0:T(8,128)(2,1)S(1)}, u32[]{:S(2)}, u32[]{:S(2)}) collective-permute-start(bf16[16,2048]{1,0:T(8,128)(2,1)} %shard_map.78), channel_id=1, source_target_pairs={{0,128},{16,144},{32,160},{48,176},{64,192},{80,208},{96,224},{112... | collective-permute-start | bytes 196616 | tf_op jit(solution)/shard_map/ppermute | solution.py:202
  12.0 4.9 %copy-start.2 = (bf16[16,2048]{1,0:T(8,128)(2,1)S(1)}, bf16[16,2048]{1,0:T(8,128)(2,1)}, u32[]{:S(2)}) copy-start(bf16[16,2048]{1,0:T(8,128)(2,1)} %shard_map.78) | copy-start | bytes 196612
  12.0 74.5 %copy-start = (bf16[2048,768]{1,0:T(8,128)(2,1)S(1)}, bf16[2048,768]{1,0:T(8,128)(2,1)}, u32[]{:S(2)}) copy-start(bf16[2048,768]{1,0:T(8,128)(2,1)} %proj_ref.1) | copy-start | bytes 9437188
  12.0 74.5 %copy-start.1 = (f32[12288]{0:T(1024)S(1)}, f32[12288]{0:T(1024)}, u32[]{:S(2)}) copy-start(f32[12288]{0:T(1024)} %param.10) | copy-start | bytes 147460
  12.0 57.8 %all-to-all-start = ((bf16[16,960,128]{2,1,0:T(8,128)(2,1)}), bf16[16,960,128]{2,1,0:T(8,128)(2,1)}, u32[]{:S(2)}, u32[]{:S(2)}) async-start(bf16[16,960,128]{2,1,0:T(8,128)(2,1)} %shard_map.77), calls=%async_computation | async-start | bytes 7864320 | tf_op jit(solution)/shard_map/all_to_all | solution.py:217
  16.9 4.8 %collective-permute-start.3 = (bf16[16,2048]{1,0:T(8,128)(2,1)S(1)}, bf16[16,2048]{1,0:T(8,128)(2,1)S(1)}, u32[]{:S(2)}, u32[]{:S(2)}) collective-permute-start(bf16[16,2048]{1,0:T(8,128)(2,1)S(1)} %add.20), channel_id=1, source_target_pairs={{0,48},{16,32},{32,16},{48,0},{64,112},{80,96},{96,80},{112,64},{1... | collective-permute-start | bytes 196616 | tf_op jit(solution)/shard_map/ppermute | solution.py:202
  18.9 6.0 %collective-permute-start.2 = (bf16[16,2048]{1,0:T(8,128)(2,1)S(1)}, bf16[16,2048]{1,0:T(8,128)(2,1)S(1)}, u32[]{:S(2)}, u32[]{:S(2)}) collective-permute-start(bf16[16,2048]{1,0:T(8,128)(2,1)S(1)} %add.20), channel_id=1, source_target_pairs={{0,32},{16,48},{32,0},{48,16},{64,96},{80,112},{96,64},{112,80},{1... | collective-permute-start | bytes 196616 | tf_op jit(solution)/shard_map/ppermute | solution.py:202
  20.4 6.5 %collective-permute-start.1 = (bf16[16,2048]{1,0:T(8,128)(2,1)S(1)}, bf16[16,2048]{1,0:T(8,128)(2,1)S(1)}, u32[]{:S(2)}, u32[]{:S(2)}) collective-permute-start(bf16[16,2048]{1,0:T(8,128)(2,1)S(1)} %add.20), channel_id=1, source_target_pairs={{0,16},{16,0},{32,48},{48,32},{64,80},{80,64},{96,112},{112,96},{1... | collective-permute-start | bytes 196616 | tf_op jit(solution)/shard_map/ppermute | solution.py:202
  27.0 9.7 %collective-permute-start.4 = (bf16[16,2048]{1,0:T(8,128)(2,1)S(1)}, bf16[16,2048]{1,0:T(8,128)(2,1)S(1)}, u32[]{:S(2)}, u32[]{:S(2)}) collective-permute-start(bf16[16,2048]{1,0:T(8,128)(2,1)S(1)} %add_add_fusion), channel_id=1, source_target_pairs={{0,64},{16,80},{32,96},{48,112},{64,0},{80,16},{96,32},{112,48},{1... | collective-permute-start | bytes 196616 | tf_op jit(solution)/shard_map/ppermute | solution.py:202
  84.2 2.3 %collective-permute-start.5 = (bf16[8,16,2048]{2,1,0:T(8,128)(2,1)}, bf16[8,16,2048]{2,1,0:T(8,128)(2,1)}, u32[]{:S(2)}, u32[]{:S(2)}) collective-permute-start(bf16[8,16,2048]{2,1,0:T(8,128)(2,1)} %all_to_all.20.own_ref), channel_id=1, source_target_pairs={{0,1},{1,0},{2,3},{3,2},{4,5},{5,4},{6,7},{7,6},{8,9},{9,8},{10,11... | collective-permute-start | bytes 1572872 | tf_op jit(solution)/shard_map/ppermute | solution.py:202
  91.1 3.0 %collective-permute-start.6 = (f32[8,16,2048]{2,1,0:T(8,128)S(1)}, f32[8,16,2048]{2,1,0:T(8,128)S(1)}, u32[]{:S(2)}, u32[]{:S(2)}) collective-permute-start(f32[8,16,2048]{2,1,0:T(8,128)S(1)} %get-tuple-element.15), channel_id=1, source_target_pairs={{0,1},{1,0},{2,3},{3,2},{4,5},{5,4},{6,7},{7,6},{8,9},{9,8},{10,11... | collective-permute-start | bytes 3145736 | tf_op jit(solution)/shard_map/ppermute | solution.py:202
  91.3 2.8 %collective-permute-start.7 = (bf16[8,16,768]{2,1,0:T(8,128)(2,1)S(1)}, bf16[8,16,768]{2,1,0:T(8,128)(2,1)S(1)}, u32[]{:S(2)}, u32[]{:S(2)}) collective-permute-start(bf16[8,16,768]{2,1,0:T(8,128)(2,1)S(1)} %get-tuple-element.17), channel_id=1, source_target_pairs={{0,1},{1,0},{2,3},{3,2},{4,5},{5,4},{6,7},{7,6},{8,9},{9,8},{10,11... | collective-permute-start | bytes 589832 | tf_op jit(solution)/shard_map/ppermute | solution.py:202
  114.1 19.4 %all-to-all-start.3 = ((f32[16,16,128]{2,1,0:T(8,128)}), f32[16,16,128]{2,1,0:T(8,128)S(1)}, u32[]{:S(2)}, u32[]{:S(2)}) async-start(f32[16,16,128]{2,1,0:T(8,128)} %shard_map.82), calls=%async_computation.3 | async-start | bytes 262144 | tf_op jit(solution)/shard_map/all_to_all | solution.py:251

commit v3 on v2

--- a/solution.py
+++ b/solution.py
@@ -22,37 +22,68 @@
     return pl.CostEstimate(flops=flops, bytes_accessed=nbytes, transcendentals=0)
 
 
-def pack_kernel(dests, obs_ref, prior_ref, out_ref):
-    sub = obs_ref.shape[0] // dests
+def pack_kernel(chips, core_ref, obs_ref, prior_ref, keep_ref, give_ref):
+    sub = obs_ref.shape[0] // (2 * chips)
     evo = prior_ref.shape[0]
-    for d in range(dests):
-        out_ref[d, :sub] = obs_ref[d * sub : (d + 1) * sub]
-        for l in range(sub // LANES):
-            at = d * sub + l * LANES
-            value = prior_ref[:, at : at + LANES]
-            high = value.astype(BF16)
-            row = sub + l * 2 * evo
-            out_ref[d, row : row + evo] = high
-            out_ref[d, row + evo : row + 2 * evo] = (value - high.astype(F32)).astype(BF16)
-
-
-def pack(obs, prior_t, n_col):
+    for m in range(chips):
+        for side, out_ref in enumerate((keep_ref, give_ref)):
+            start = pl.multiple_of((2 * m + jnp.bitwise_xor(core_ref[0], side)) * sub, LANES)
+            out_ref[m, :sub] = obs_ref[pl.ds(start, sub)]
+            for l in range(sub // LANES):
+                value = prior_ref[:, pl.ds(pl.multiple_of(start + l * LANES, LANES), LANES)]
+                high = value.astype(BF16)
+                row = sub + l * 2 * evo
+                out_ref[m, row : row + evo] = high
+                out_ref[m, row + evo : row + 2 * evo] = (value - high.astype(F32)).astype(BF16)
+
+
+def pack(core, obs, prior_t, n_col):
     rows, width = obs.shape
     evo = prior_t.shape[0]
     sub = rows // n_col
     depth = sub + 2 * evo * sub // LANES
-    dests = 4
-    return pl.pallas_call(
-        functools.partial(pack_kernel, dests),
-        out_shape=jax.ShapeDtypeStruct((n_col, depth, width), BF16),
-        grid=(n_col // dests,),
+    chips = 2
+    block = pl.BlockSpec((chips, depth, width), lambda i, _: (i, 0, 0))
+    return pl.pallas_call(
+        functools.partial(pack_kernel, chips),
+        out_shape=[jax.ShapeDtypeStruct((n_col // 2, depth, width), BF16)] * 2,
+        grid_spec=pltpu.PrefetchScalarGridSpec(
+            num_scalar_prefetch=1,
+            grid=(n_col // 2 // chips,),
+            in_specs=[
+                pl.BlockSpec((2 * chips * sub, width), lambda i, _: (i, 0)),
+                pl.BlockSpec((evo, 2 * chips * sub), lambda i, _: (0, i)),
+            ],
+            out_specs=[block] * 2,
+        ),
+        cost_estimate=cost(0, 2 * 2 * n_col * depth * width),
+    )(core, obs, prior_t)
+
+
+def join_kernel(got_ref, picked_ref, out_ref):
+    chips, depth, width = got_ref.shape
+    evo, count = picked_ref.shape
+    out_ref[:, :depth] = got_ref[...]
+    for l in range(count // width):
+        tile = picked_ref[:, l * width : (l + 1) * width]
+        for m in range(chips):
+            out_ref[m, depth + l * evo : depth + (l + 1) * evo] = tile
+
+
+def join(got, picked):
+    chips, depth, width = got.shape
+    more = picked.size // width
+    return pl.pallas_call(
+        join_kernel,
+        out_shape=jax.ShapeDtypeStruct((chips, depth + more, width), BF16),
+        grid=(chips // 2,),
         in_specs=[
-            pl.BlockSpec((dests * sub, width), lambda i: (i, 0)),
-            pl.BlockSpec((evo, dests * sub), lambda i: (0, i)),
+            pl.BlockSpec((2, depth, width), lambda i: (i, 0, 0)),
+            pl.BlockSpec(picked.shape, lambda i: (0, 0)),
         ],
-        out_specs=pl.BlockSpec((dests, depth, width), lambda i: (i, 0, 0)),
-        cost_estimate=cost(0, 2 * 2 * n_col * depth * width),
-    )(obs, prior_t)
+        out_specs=pl.BlockSpec((2, depth + more, width), lambda i: (i, 0, 0)),
+        cost_estimate=cost(0, 4 * chips * (depth + more) * width),
+    )(got, picked)
 
 
 def pick_kernel(first_ref, idx_ref, sky_ref, out_ref):
@@ -95,22 +126,28 @@
 
 
 def main_kernel(
-    me_ref, msg_ref, own_ref, other_ref, apod_ref, proj_ref, p_own, p_other, s_own, s_other, panel, weighted
+    me_ref, near_ref, far_ref, other_ref, apod_ref, proj_ref, p_own, p_other, s_own, s_other, panel, weighted
 ):
-    chips, evo, count = own_ref.shape
+    chips, evo, _ = p_own.shape
     prows, sub = proj_ref.shape
     me = me_ref[0]
     core = me % 2
     half = chips * evo
-    for m in range(chips):
-        panel[m * evo : (m + 1) * evo] = own_ref[m]
-        panel[half + m * evo : half + (m + 1) * evo] = other_ref[m]
-    sources = [2 * m + jnp.bitwise_xor(core, b) for b in range(2) for m in range(chips)]
+    depth = near_ref.shape[1]
+    for k in range(chips):
+        for side in range(2):
+            tile = (2 * k + jnp.bitwise_xor(core, side)) * evo
+            lanes = slice((2 * k + side) * LANES, (2 * k + side + 1) * LANES)
+            for m in range(chips):
+                panel[m * evo : (m + 1) * evo, lanes] = far_ref[m, pl.ds(pl.multiple_of(depth + tile, evo), evo)]
+                panel[half + m * evo : half + (m + 1) * evo, lanes] = other_ref[
+                    m, pl.ds(pl.multiple_of(tile, evo), evo)
+                ]
     for n in range(sub // WIDE):
         rows = slice(n * WIDE, (n + 1) * WIDE)
         added = jnp.zeros((2 * half, WIDE), F32)
         for k in range(chips):
-            obs = jnp.concatenate([msg_ref[2 * k, rows], msg_ref[2 * k + 1, rows]], axis=1)
+            obs = jnp.concatenate([near_ref[k, rows], far_ref[k, rows]], axis=1)
             added += lax.dot_general(
                 panel[:, k * WIDE : (k + 1) * WIDE], obs, NT, preferred_element_type=F32
             )
@@ -121,8 +158,9 @@
             row = sub + block * 2 * evo
             prior = jnp.concatenate(
                 [
-                    msg_ref[s, row : row + evo].astype(F32) + msg_ref[s, row + evo : row + 2 * evo].astype(F32)
-                    for s in sources
+                    ref[m, row : row + evo].astype(F32) + ref[m, row + evo : row + 2 * evo].astype(F32)
+                    for ref in (near_ref, far_ref)
+                    for m in range(chips)
                 ],
                 axis=0,
             )
@@ -136,8 +174,8 @@
         p_other[:, :, cols] = part[half:].reshape(chips, evo, WIDE)
 
 
-def main_step(me, msg, own, other, apod, proj):
-    chips, evo, count = own.shape
+def main_step(me, near, far, other, apod, proj, evo, count):
+    chips = near.shape[0]
     prows, sub = proj.shape
     total = 2 * chips * evo
     return pl.pallas_call(
@@ -152,8 +190,8 @@
         out_specs=tuple(whole(4)),
         scratch_shapes=[pltpu.VMEM((total, count), BF16), pltpu.VMEM((total, sub), BF16)],
         compiler_params=pltpu.CompilerParams(vmem_limit_bytes=28 * MIB),
-        cost_estimate=cost(2 * total * sub * (count + prows), 2 * msg.size + 2 * proj.size + 4 * total * prows),
-    )(me, msg, own, other, apod, proj)
+        cost_estimate=cost(2 * total * sub * (count + prows), 4 * near.size + 2 * proj.size + 4 * total * prows),
+    )(me, near, far, other, apod, proj)
 
 
 def home_kernel(p_own, p_got, s_own, s_got, out_ref):
@@ -178,24 +216,6 @@
             at = pl.ds(pl.multiple_of((2 * m + jnp.bitwise_xor(core, b)) * sub, LANES), sub)
             came = msg_ref[m, :, prows + b * sub : prows + (b + 1) * sub].astype(F32)
             out_ref[:, at] = prior_ref[:, at] + came
-
-
-EARLY, LATE = (3, 5, 6, 7, 2), (1, 4)
-
-
-def stack_kernel(*refs):
-    for n, ref in enumerate(refs[:-1]):
-        refs[-1][n] = ref[...]
-
-
-def stack(parts):
-    return pl.pallas_call(
-        stack_kernel,
-        out_shape=jax.ShapeDtypeStruct((len(parts), *parts[0].shape), parts[0].dtype),
-        in_specs=whole(len(parts)),
-        out_specs=whole(1)[0],
-        cost_estimate=cost(0, 4 * len(parts) * parts[0].size),
-    )(*parts)
 
 
 def swap(x, axis, bits, n):
@@ -213,21 +233,26 @@
     first = (lax.axis_index("row") * rows_blk).astype(jnp.int32)
     picked = pick(first.reshape(1), idx.reshape(1, count), skies.T)
     far = swap(picked, "row", n_row // 2, n_row)
-    packed, far = lax.optimization_barrier((pack(obs, prior_t, n_col), far))
-    msg = lax.all_to_all(packed, "col", 0, 0, tiled=True)
+    keep, give = pack((me % 2).reshape(1), obs, prior_t, n_col)
+    keep, give, far = lax.optimization_barrier((keep, give, far))
+    same = [[2 * m + b for m in range(chips)] for b in range(2)]
+    to_chips = functools.partial(
+        lax.all_to_all, axis_name="col", split_axis=0, concat_axis=0, tiled=True, axis_index_groups=same
+    )
+    near_rows = to_chips(keep)
+    got = swap(give, "col", 1, n_col)
     picked = picked + far
     for group in ((1, 2, 3), (4,)):
         parts = [swap(picked, "row", k, n_row) for k in group]
         for part in parts:
             picked = picked + part
-    copies = jnp.broadcast_to(picked[None], (chips, evo, count))
-    msg, copies = lax.optimization_barrier((msg, copies))
-    same = [[2 * m + b for m in range(chips)] for b in range(2)]
-    own = lax.all_to_all(copies, "col", 0, 0, tiled=True, axis_index_groups=same)
-    other = swap(own, "col", 1, n_col)
+    joined = join(got, picked)
+    near_rows, joined = lax.optimization_barrier((near_rows, joined))
+    far_rows = to_chips(joined)
+    other = swap(far_rows[:, keep.shape[1] :], "col", 1, n_col)
 
     p_own, p_other, s_own, s_other = main_step(
-        me.reshape(1), msg, own, other, apod.reshape(rows_blk // LANES, LANES), proj
+        me.reshape(1), near_rows, far_rows, other, apod.reshape(rows_blk // LANES, LANES), proj, evo, count
     )
     p_got = swap(p_other, "col", 1, n_col)
     s_got = swap(s_other, "col", 1, n_col)
@@ -239,8 +264,7 @@
         compiler_params=pltpu.CompilerParams(vmem_limit_bytes=16 * MIB),
         cost_estimate=cost(p_own.size, 10 * p_own.size),
     )(p_own, p_got, s_own, s_got)
-    same = [[2 * m + b for m in range(chips)] for b in range(2)]
-    home = lax.all_to_all(home, "col", 0, 0, tiled=True, axis_index_groups=same)
+    home = to_chips(home)
     share = pl.pallas_call(
         sum_kernel,
         out_shape=jax.ShapeDtypeStruct((n_row, evo, prows // n_row), F32),

time: 135 us -> 129 us (0.956)
  waiting for transfers between devices: 55.3 us -> 23.6 us
  blocking collectives: 32.3 us -> 56.6 us
  Pallas kernels: 17.1 us -> 18.7 us
    all_to_all x1, waiting for transfers between devices: 33.2 us -> 2.13 us  [on_device(): near_rows = to_chips(keep)]
    all_to_all x2, blocking collectives: 32.3 us -> 56.6 us  [the longest x1 38.6 us: on_device(): far_rows = to_chips(joined)]
    pallas_call x1 -> x2, Pallas kernels: 4.51 us -> 8.43 us  [the longest x1 4.57 us: pack(): pl.pallas_call(functools.partial(pack_kernel, chips), out_shape=[jax.Shap...]
    pallas_call x1, Pallas kernels: 4.56 us -> 2.22 us  [main_step(): pl.pallas_call(main_kernel, out_shape=(jax.ShapeDtypeStruct((chips, evo,...]
    ppermute x8 -> x9, waiting for transfers between devices: 15 us -> 14.4 us  [swap(): return lax.ppermute(x, axis, [(i, i ^ bits) for i in range(n)])]
    ppermute x8 -> x9, starting transfers between devices: 13.2 us -> 13.4 us  [swap(): return lax.ppermute(x, axis, [(i, i ^ bits) for i in range(n)])]
  transfers between devices with their start and end apart: 10 -> 11, of which waited for: 7 -> 7; matrix products, arithmetic and copies ran while one was open for 0% -> 1% of each run, Pallas kernels for 5% -> 8%
where the time goes in v3:
time: 129 us
  blocking collectives  56.6 us (44%)
  starting transfers between devices  27.8 us (22%)
  waiting for transfers between devices  23.6 us (18%)
  Pallas kernels  18.7 us (14%)
  other arithmetic  1.3 us (1%)
    all_to_all x1, blocking collectives, on_device(): far_rows = to_chips(joined)  38.6 us
    all_to_all x1, blocking collectives, on_device(): home = to_chips(home)  18 us
    ppermute x9, waiting for transfers between devices, swap(): return lax.ppermute(x, axis, [(i, i ^ bits) for i in range(n)])  14.4 us
    ppermute x9, starting transfers between devices, swap(): return lax.ppermute(x, axis, [(i, i ^ bits) for i in range(n)])  13.4 us
    all_to_all x1, starting transfers between devices, on_device(): share = lax.all_to_all(share, 'row', 0, 0, tiled=True)  10 us
    all_to_all x1, waiting for transfers between devices, on_device(): share = lax.all_to_all(share, 'row', 0, 0, tiled=True)  7.1 us
    pallas_call x1, Pallas kernels, pack(): pl.pallas_call(functools.partial(pack_kernel, chips), out_shape=[jax.Shap...  4.57 us
    all_to_all x1, starting transfers between devices, on_device(): near_rows = to_chips(keep)  4.43 us
  transfers between devices with their start and end apart: 11, of which 7 were waited for; matrix products, arithmetic and copies ran while one was open for 1% of the time, Pallas kernels for 8%

profile of v3, /device:TPU:32, one launch (start us, length us, event | category | flops | bytes accessed | tf_op | source)
XLA Modules:
  0.0 128.8 jit_solution(4083083579818058166)
XLA Ops:
  0.6 3.7 %shard_map.78 = bf16[16,2048]{1,0:T(8,128)(2,1)} custom-call(s32[1]{0:T(128)} %bitcast.3.first_ref, s32[1,2048]{1,0:T(1,128)} %bitcast.15, bf16[16,12288]{1,0:T(8,128)(2,1)} %bitcast.14), custom_call_target="tpu_custom_call" | custom-call | flops 805306368 | bytes 458752 | tf_op jit(solution)/shard_map/pallas_call | solution.py:112
  4.3 3.2 %collective-permute-start = (bf16[16,2048]{1,0:T(8,128)(2,1)}, bf16[16,2048]{1,0:T(8,128)(2,1)S(1)}, u32[]{:S(2)}, u32[]{:S(2)}) collective-permute-start(bf16[16,2048]{1,0:T(8,128)(2,1)} %shard_map.78), channel_id=1, source_target_pairs={{0,128},{16,144},{32,160},{48,176},{64,192},{80,208},{96,224},{112... | collective-permute-start | bytes 196616 | tf_op jit(solution)/shard_map/ppermute | solution.py:222
  7.5 4.6 %shard_map.77 = (bf16[8,960,128]{2,1,0:T(8,128)(2,1)}, bf16[8,960,128]{2,1,0:T(8,128)(2,1)}) custom-call(s32[1]{0:T(128)} %bitcast.core_ref, bf16[12288,128]{1,0:T(8,128)(2,1)} %obs_ref.1, f32[16,12288]{1,0:T(8,128)} %bitcast.10), custom_call_target="tpu_custom_call" | custom-call | bytes 7864320 | tf_op jit(solution)/shard_map/pallas_call | solution.py:47
  12.1 0.0 collective-permute-done
  12.1 0.1 collective-permute-start.1
  12.2 4.4 %all-to-all-start = ((bf16[8,960,128]{2,1,0:T(8,128)(2,1)}), bf16[8,960,128]{2,1,0:T(8,128)(2,1)S(1)}, u32[]{:S(2)}, u32[]{:S(2)}) async-start(bf16[8,960,128]{2,1,0:T(8,128)(2,1)} %get-tuple-element.15), calls=%async_computation | async-start | bytes 3932160 | tf_op jit(solution)/shard_map/all_to_all | solution.py:242
  16.6 2.0 %collective-permute-start.4 = (bf16[16,2048]{1,0:T(8,128)(2,1)S(1)}, bf16[16,2048]{1,0:T(8,128)(2,1)S(1)}, u32[]{:S(2)}, u32[]{:S(2)}) collective-permute-start(bf16[16,2048]{1,0:T(8,128)(2,1)S(1)} %add.21), channel_id=1, source_target_pairs={{0,48},{16,32},{32,16},{48,0},{64,112},{80,96},{96,80},{112,64},{1... | collective-permute-start | bytes 196616 | tf_op jit(solution)/shard_map/ppermute | solution.py:222
  18.7 1.5 %collective-permute-start.3 = (bf16[16,2048]{1,0:T(8,128)(2,1)S(1)}, bf16[16,2048]{1,0:T(8,128)(2,1)S(1)}, u32[]{:S(2)}, u32[]{:S(2)}) collective-permute-start(bf16[16,2048]{1,0:T(8,128)(2,1)S(1)} %add.21), channel_id=1, source_target_pairs={{0,32},{16,48},{32,0},{48,16},{64,96},{80,112},{96,64},{112,80},{1... | collective-permute-start | bytes 196616 | tf_op jit(solution)/shard_map/ppermute | solution.py:222
  20.1 1.4 %collective-permute-start.2 = (bf16[16,2048]{1,0:T(8,128)(2,1)S(1)}, bf16[16,2048]{1,0:T(8,128)(2,1)S(1)}, u32[]{:S(2)}, u32[]{:S(2)}) collective-permute-start(bf16[16,2048]{1,0:T(8,128)(2,1)S(1)} %add.21), channel_id=1, source_target_pairs={{0,16},{16,0},{32,48},{48,32},{64,80},{80,64},{96,112},{112,96},{1... | collective-permute-start | bytes 196616 | tf_op jit(solution)/shard_map/ppermute | solution.py:222
  21.5 0.0 collective-permute-done.4
  21.5 3.0 %collective-permute-done.3 = bf16[16,2048]{1,0:T(8,128)(2,1)S(1)} collective-permute-done((bf16[16,2048]{1,0:T(8,128)(2,1)S(1)}, bf16[16,2048]{1,0:T(8,128)(2,1)S(1)}, u32[]{:S(2)}, u32[]{:S(2)}) %collective-permute-start.3) | collective-permute-done | bytes 65568 | tf_op jit(solution)/shard_map/ppermute | solution.py:222
  24.4 2.0 %collective-permute-done.2 = bf16[16,2048]{1,0:T(8,128)(2,1)S(1)} collective-permute-done((bf16[16,2048]{1,0:T(8,128)(2,1)S(1)}, bf16[16,2048]{1,0:T(8,128)(2,1)S(1)}, u32[]{:S(2)}, u32[]{:S(2)}) %collective-permute-start.2) | collective-permute-done | bytes 65568 | tf_op jit(solution)/shard_map/ppermute | solution.py:222
  26.5 4.6 %collective-permute-start.5 = (bf16[16,2048]{1,0:T(8,128)(2,1)S(1)}, bf16[16,2048]{1,0:T(8,128)(2,1)S(1)}, u32[]{:S(2)}, u32[]{:S(2)}) collective-permute-start(bf16[16,2048]{1,0:T(8,128)(2,1)S(1)} %add_add_fusion), channel_id=1, source_target_pairs={{0,64},{16,80},{32,96},{48,112},{64,0},{80,16},{96,32},{112,48},{1... | collective-permute-start | bytes 196616 | tf_op jit(solution)/shard_map/ppermute | solution.py:222
  31.1 5.1 %collective-permute-done.5 = bf16[16,2048]{1,0:T(8,128)(2,1)S(1)} collective-permute-done((bf16[16,2048]{1,0:T(8,128)(2,1)S(1)}, bf16[16,2048]{1,0:T(8,128)(2,1)S(1)}, u32[]{:S(2)}, u32[]{:S(2)}) %collective-permute-start.5) | collective-permute-done | bytes 65568 | tf_op jit(solution)/shard_map/ppermute | solution.py:222
  36.1 0.6 add.25.picked_ref
  36.8 0.0 collective-permute-done.1.got_ref
  36.8 3.9 %shard_map.79 = bf16[8,1216,128]{2,1,0:T(8,128)(2,1)} custom-call(bf16[8,960,128]{2,1,0:T(8,128)(2,1)} %collective-permute-done.1.got_ref, bf16[16,2048]{1,0:T(8,128)(2,1)} %add.25.picked_ref), custom_call_target="tpu_custom_call" | custom-call | bytes 4980736 | tf_op jit(solution)/shard_map/pallas_call | solution.py:76
  40.7 2.1 %all-to-all-done.near_ref = bf16[8,960,128]{2,1,0:T(8,128)(2,1)S(1)} async-done(((bf16[8,960,128]{2,1,0:T(8,128)(2,1)}), bf16[8,960,128]{2,1,0:T(8,128)(2,1)S(1)}, u32[]{:S(2)}, u32[]{:S(2)}) %all-to-all-start) | async-done | bytes 1966112 | tf_op jit(solution)/shard_map/all_to_all | solution.py:242
  42.8 38.6 %all_to_all.20.far_ref = bf16[8,1216,128]{2,1,0:T(8,128)(2,1)S(1)} all-to-all(bf16[8,1216,128]{2,1,0:T(8,128)(2,1)} %shard_map.79), channel_id=1, replica_groups={{0,2,4,6,8,10,12,14},{1,3,5,7,9,11,13,15},{16,18,20,22,24,26,28,30},{17..., dimensions={0} | all-to-all | bytes 4980736 | tf_op jit(solution)/shard_map/all_to_all | solution.py:251
  81.4 0.1 collective-permute-start.6
  81.5 1.9 %collective-permute-done.6.other_ref = bf16[8,256,128]{2,1,0:T(8,128)(2,1)S(1)} collective-permute-done((bf16[8,256,128]{2,1,0:T(8,128)(2,1)S(1)}, bf16[8,256,128]{2,1,0:T(8,128)(2,1)S(1)}, u32[]{:S(2)}, u32[]{:S(2)}) %collective-permute-start.6) | collective-permute-done | bytes 524320 | tf_op jit(solution)/shard_map/ppermute | solution.py:222
  83.4 2.2 %shard_map.80 = (f32[8,16,2048]{2,1,0:T(8,128)S(1)}, f32[8,16,2048]{2,1,0:T(8,128)S(1)}, bf16[8,16,768]{2,1,0:T(8,128)(2,1)S(1)}, bf16[8,16,768]{2,1,0:T(8,128)(2,1)S(1)}) custom-call(s32[1]{0:T(128)} %bitcast.1.me_ref, bf16[8,960,128]{2,1,0:T(8,128)(2,1)S(1)} %all-to-all-done.near_ref, bf16[8,1216,128]{2,1,0:T(8,128)(2,1)S(1)} %all_to_all.20.far_ref, ...), custom_call_target="tpu_custom_call" | custom-call | flops 1610612736 | bytes 9175040 | tf_op jit(solution)/shard_map/pallas_call | solution.py:181
  85.7 0.2 collective-permute-start.7
  85.9 0.4 collective-permute-start.8
  86.3 2.4 %collective-permute-done.8.s_got = bf16[8,16,768]{2,1,0:T(8,128)(2,1)S(1)} collective-permute-done((bf16[8,16,768]{2,1,0:T(8,128)(2,1)S(1)}, bf16[8,16,768]{2,1,0:T(8,128)(2,1)S(1)}, u32[]{:S(2)}, u32[]{:S(2)}) %collective-permute-start.8) | collective-permute-done | bytes 196640 | tf_op jit(solution)/shard_map/ppermute | solution.py:222
  88.7 0.1 shard_map.81
  88.8 18.0 %all_to_all.21.msg_ref = bf16[8,16,3584]{2,1,0:T(8,128)(2,1)} all-to-all(bf16[8,16,3584]{2,1,0:T(8,128)(2,1)S(1)} %shard_map.81), channel_id=1, replica_groups={{0,2,4,6,8,10,12,14},{1,3,5,7,9,11,13,15},{16,18,20,22,24,26,28,30},{17..., dimensions={0} | all-to-all | bytes 1835008 | tf_op jit(solution)/shard_map/all_to_all | solution.py:267
  106.8 1.9 %shard_map.83 = f32[16,16,128]{2,1,0:T(8,128)} custom-call(bf16[8,16,3584]{2,1,0:T(8,128)(2,1)} %all_to_all.21.msg_ref), custom_call_target="tpu_custom_call" | custom-call | flops 458752 | bytes 917504 | tf_op jit(solution)/shard_map/pallas_call | solution.py:268
  108.7 10.0 %all-to-all-start.3 = ((f32[16,16,128]{2,1,0:T(8,128)}), f32[16,16,128]{2,1,0:T(8,128)S(1)}, u32[]{:S(2)}, u32[]{:S(2)}) async-start(f32[16,16,128]{2,1,0:T(8,128)} %shard_map.83), calls=%async_computation.3 | async-start | bytes 262144 | tf_op jit(solution)/shard_map/all_to_all | solution.py:275
  118.7 2.4 %shard_map.82 = f32[16,12288]{1,0:T(8,128)} custom-call(s32[1]{0:T(128)} %bitcast.core_ref, bf16[8,16,3584]{2,1,0:T(8,128)(2,1)} %all_to_all.21.msg_ref, f32[16,12288]{1,0:T(8,128)} %bitcast.11), custom_call_target="tpu_custom_call" | custom-call | flops 196608 | bytes 1966080 | tf_op jit(solution)/shard_map/pallas_call | solution.py:277
  121.1 7.1 %all-to-all-done.3 = f32[16,16,128]{2,1,0:T(8,128)S(1)} async-done(((f32[16,16,128]{2,1,0:T(8,128)}), f32[16,16,128]{2,1,0:T(8,128)S(1)}, u32[]{:S(2)}, u32[]{:S(2)}) %all-to-all-start.3) | async-done | bytes 131104 | tf_op jit(solution)/shard_map/all_to_all | solution.py:275
  128.2 0.6 reduce_sum.9
  (10 shorter events, 0.1 us)
Async XLA Ops:
  4.3 7.8 %collective-permute-start = (bf16[16,2048]{1,0:T(8,128)(2,1)}, bf16[16,2048]{1,0:T(8,128)(2,1)S(1)}, u32[]{:S(2)}, u32[]{:S(2)}) collective-permute-start(bf16[16,2048]{1,0:T(8,128)(2,1)} %shard_map.78), channel_id=1, source_target_pairs={{0,128},{16,144},{32,160},{48,176},{64,192},{80,208},{96,224},{112... | collective-permute-start | bytes 196616 | tf_op jit(solution)/shard_map/ppermute | solution.py:222
  12.1 4.5 %copy-start.2 = (bf16[16,2048]{1,0:T(8,128)(2,1)S(1)}, bf16[16,2048]{1,0:T(8,128)(2,1)}, u32[]{:S(2)}) copy-start(bf16[16,2048]{1,0:T(8,128)(2,1)} %shard_map.78) | copy-start | bytes 196612
  12.1 24.7 %collective-permute-start.1 = (bf16[8,960,128]{2,1,0:T(8,128)(2,1)}, bf16[8,960,128]{2,1,0:T(8,128)(2,1)}, u32[]{:S(2)}, u32[]{:S(2)}) collective-permute-start(bf16[8,960,128]{2,1,0:T(8,128)(2,1)} %get-tuple-element.16), channel_id=1, source_target_pairs={{0,1},{1,0},{2,3},{3,2},{4,5},{5,4},{6,7},{7,6},{8,9},{9,8},{10,11... | collective-permute-start | bytes 5898248 | tf_op jit(solution)/shard_map/ppermute | solution.py:222
  12.2 30.6 %all-to-all-start = ((bf16[8,960,128]{2,1,0:T(8,128)(2,1)}), bf16[8,960,128]{2,1,0:T(8,128)(2,1)S(1)}, u32[]{:S(2)}, u32[]{:S(2)}) async-start(bf16[8,960,128]{2,1,0:T(8,128)(2,1)} %get-tuple-element.15), calls=%async_computation | async-start | bytes 3932160 | tf_op jit(solution)/shard_map/all_to_all | solution.py:242
  16.6 4.8 %collective-permute-start.4 = (bf16[16,2048]{1,0:T(8,128)(2,1)S(1)}, bf16[16,2048]{1,0:T(8,128)(2,1)S(1)}, u32[]{:S(2)}, u32[]{:S(2)}) collective-permute-start(bf16[16,2048]{1,0:T(8,128)(2,1)S(1)} %add.21), channel_id=1, source_target_pairs={{0,48},{16,32},{32,16},{48,0},{64,112},{80,96},{96,80},{112,64},{1... | collective-permute-start | bytes 196616 | tf_op jit(solution)/shard_map/ppermute | solution.py:222
  18.7 5.8 %collective-permute-start.3 = (bf16[16,2048]{1,0:T(8,128)(2,1)S(1)}, bf16[16,2048]{1,0:T(8,128)(2,1)S(1)}, u32[]{:S(2)}, u32[]{:S(2)}) collective-permute-start(bf16[16,2048]{1,0:T(8,128)(2,1)S(1)} %add.21), channel_id=1, source_target_pairs={{0,32},{16,48},{32,0},{48,16},{64,96},{80,112},{96,64},{112,80},{1... | collective-permute-start | bytes 196616 | tf_op jit(solution)/shard_map/ppermute | solution.py:222
  20.1 6.4 %collective-permute-start.2 = (bf16[16,2048]{1,0:T(8,128)(2,1)S(1)}, bf16[16,2048]{1,0:T(8,128)(2,1)S(1)}, u32[]{:S(2)}, u32[]{:S(2)}) collective-permute-start(bf16[16,2048]{1,0:T(8,128)(2,1)S(1)} %add.21), channel_id=1, source_target_pairs={{0,16},{16,0},{32,48},{48,32},{64,80},{80,64},{96,112},{112,96},{1... | collective-permute-start | bytes 196616 | tf_op jit(solution)/shard_map/ppermute | solution.py:222
  26.5 9.6 %collective-permute-start.5 = (bf16[16,2048]{1,0:T(8,128)(2,1)S(1)}, bf16[16,2048]{1,0:T(8,128)(2,1)S(1)}, u32[]{:S(2)}, u32[]{:S(2)}) collective-permute-start(bf16[16,2048]{1,0:T(8,128)(2,1)S(1)} %add_add_fusion), channel_id=1, source_target_pairs={{0,64},{16,80},{32,96},{48,112},{64,0},{80,16},{96,32},{112,48},{1... | collective-permute-start | bytes 196616 | tf_op jit(solution)/shard_map/ppermute | solution.py:222
  40.7 42.8 %copy-start.1 = (f32[12288]{0:T(1024)S(1)}, f32[12288]{0:T(1024)}, u32[]{:S(2)}) copy-start(f32[12288]{0:T(1024)} %param.10) | copy-start | bytes 147460
  42.8 40.6 %copy-start = (bf16[2048,768]{1,0:T(8,128)(2,1)S(1)}, bf16[2048,768]{1,0:T(8,128)(2,1)}, u32[]{:S(2)}) copy-start(bf16[2048,768]{1,0:T(8,128)(2,1)} %proj_ref.1) | copy-start | bytes 9437188
  81.4 2.0 %collective-permute-start.6 = (bf16[8,256,128]{2,1,0:T(8,128)(2,1)S(1)}, bf16[8,256,128]{2,1,0:T(8,128)(2,1)S(1)}, u32[]{:S(2)}, u32[]{:S(2)}) collective-permute-start(bf16[8,256,128]{2,1,0:T(8,128)(2,1)S(1)} %slice.4), channel_id=1, source_target_pairs={{0,1},{1,0},{2,3},{3,2},{4,5},{5,4},{6,7},{7,6},{8,9},{9,8},{10,11... | collective-permute-start | bytes 1572872 | tf_op jit(solution)/shard_map/ppermute | solution.py:222
  85.7 3.0 %collective-permute-start.7 = (f32[8,16,2048]{2,1,0:T(8,128)S(1)}, f32[8,16,2048]{2,1,0:T(8,128)S(1)}, u32[]{:S(2)}, u32[]{:S(2)}) collective-permute-start(f32[8,16,2048]{2,1,0:T(8,128)S(1)} %get-tuple-element.21), channel_id=1, source_target_pairs={{0,1},{1,0},{2,3},{3,2},{4,5},{5,4},{6,7},{7,6},{8,9},{9,8},{10,11... | collective-permute-start | bytes 3145736 | tf_op jit(solution)/shard_map/ppermute | solution.py:222
  85.9 2.8 %collective-permute-start.8 = (bf16[8,16,768]{2,1,0:T(8,128)(2,1)S(1)}, bf16[8,16,768]{2,1,0:T(8,128)(2,1)S(1)}, u32[]{:S(2)}, u32[]{:S(2)}) collective-permute-start(bf16[8,16,768]{2,1,0:T(8,128)(2,1)S(1)} %get-tuple-element.23), channel_id=1, source_target_pairs={{0,1},{1,0},{2,3},{3,2},{4,5},{5,4},{6,7},{7,6},{8,9},{9,8},{10,11... | collective-permute-start | bytes 589832 | tf_op jit(solution)/shard_map/ppermute | solution.py:222
  108.7 19.5 %all-to-all-start.3 = ((f32[16,16,128]{2,1,0:T(8,128)}), f32[16,16,128]{2,1,0:T(8,128)S(1)}, u32[]{:S(2)}, u32[]{:S(2)}) async-start(f32[16,16,128]{2,1,0:T(8,128)} %shard_map.83), calls=%async_computation.3 | async-start | bytes 262144 | tf_op jit(solution)/shard_map/all_to_all | solution.py:275

commit v4 on v3

--- a/solution.py
+++ b/solution.py
@@ -37,7 +37,7 @@
                 out_ref[m, row + evo : row + 2 * evo] = (value - high.astype(F32)).astype(BF16)
 
 
-def pack(core, obs, prior_t, n_col):
+def pack(core, obs, prior_t, n_col, spare):
     rows, width = obs.shape
     evo = prior_t.shape[0]
     sub = rows // n_col
@@ -46,7 +46,7 @@
     block = pl.BlockSpec((chips, depth, width), lambda i, _: (i, 0, 0))
     return pl.pallas_call(
         functools.partial(pack_kernel, chips),
-        out_shape=[jax.ShapeDtypeStruct((n_col // 2, depth, width), BF16)] * 2,
+        out_shape=[jax.ShapeDtypeStruct((n_col // 2, depth + more, width), BF16) for more in (0, spare)],
         grid_spec=pltpu.PrefetchScalarGridSpec(
             num_scalar_prefetch=1,
             grid=(n_col // 2 // chips,),
@@ -60,29 +60,31 @@
     )(core, obs, prior_t)
 
 
-def join_kernel(got_ref, picked_ref, out_ref):
-    chips, depth, width = got_ref.shape
+def join_kernel(depth, got_ref, picked_ref, out_ref, tiles, sems):
     evo, count = picked_ref.shape
-    out_ref[:, :depth] = got_ref[...]
-    for l in range(count // width):
-        tile = picked_ref[:, l * width : (l + 1) * width]
-        for m in range(chips):
-            out_ref[m, depth + l * evo : depth + (l + 1) * evo] = tile
-
-
-def join(got, picked):
-    chips, depth, width = got.shape
-    more = picked.size // width
+    for l in range(count // LANES):
+        tiles[l * evo : (l + 1) * evo] = picked_ref[:, l * LANES : (l + 1) * LANES]
+    copies = [
+        pltpu.make_async_copy(tiles, out_ref.at[m, pl.ds(depth, tiles.shape[0])], sems.at[m])
+        for m in range(out_ref.shape[0])
+    ]
+    for copy in copies:
+        copy.start()
+    for copy in copies:
+        copy.wait()
+
+
+def join(got, picked, depth):
+    chips, full, width = got.shape
+    anywhere = pl.BlockSpec(memory_space=pl.ANY)
     return pl.pallas_call(
-        join_kernel,
-        out_shape=jax.ShapeDtypeStruct((chips, depth + more, width), BF16),
-        grid=(chips // 2,),
-        in_specs=[
-            pl.BlockSpec((2, depth, width), lambda i: (i, 0, 0)),
-            pl.BlockSpec(picked.shape, lambda i: (0, 0)),
-        ],
-        out_specs=pl.BlockSpec((2, depth + more, width), lambda i: (i, 0, 0)),
-        cost_estimate=cost(0, 4 * chips * (depth + more) * width),
+        functools.partial(join_kernel, depth),
+        out_shape=jax.ShapeDtypeStruct(got.shape, BF16),
+        in_specs=[anywhere] + whole(1),
+        out_specs=anywhere,
+        scratch_shapes=[pltpu.VMEM((full - depth, width), BF16), pltpu.SemaphoreType.DMA((chips,))],
+        input_output_aliases={0: 0},
+        cost_estimate=cost(0, 2 * chips * (full - depth) * width),
     )(got, picked)
 
 
@@ -218,6 +220,21 @@
             out_ref[:, at] = prior_ref[:, at] + came
 
 
+def add_up(x, n_row):
+    ring = n_row // 2
+
+    def turn(y, by):
+        return lax.ppermute(
+            y, "row", [(h * ring + z, h * ring + (z + by) % ring) for h in range(2) for z in range(ring)]
+        )
+
+    below, above = turn(x, 1), turn(x, -1)
+    two = x + above
+    three = two + below
+    x = three + turn(three, -3) + turn(two, 3)
+    return x + swap(x, "row", ring, n_row)
+
+
 def swap(x, axis, bits, n):
     return lax.ppermute(x, axis, [(i, i ^ bits) for i in range(n)])
 
@@ -230,23 +247,19 @@
     chips = n_col // 2
     prior_t = prior.T
     me = lax.axis_index("col").astype(jnp.int32)
+    core = (me % 2).reshape(1)
     first = (lax.axis_index("row") * rows_blk).astype(jnp.int32)
-    picked = pick(first.reshape(1), idx.reshape(1, count), skies.T)
-    far = swap(picked, "row", n_row // 2, n_row)
-    keep, give = pack((me % 2).reshape(1), obs, prior_t, n_col)
-    keep, give, far = lax.optimization_barrier((keep, give, far))
     same = [[2 * m + b for m in range(chips)] for b in range(2)]
     to_chips = functools.partial(
         lax.all_to_all, axis_name="col", split_axis=0, concat_axis=0, tiled=True, axis_index_groups=same
     )
+    keep, give = pack(core, obs, prior_t, n_col, count * evo // LANES)
+    keep, give, idx = lax.optimization_barrier((keep, give, idx))
     near_rows = to_chips(keep)
+    picked = pick(first.reshape(1), idx.reshape(1, count), skies.T)
     got = swap(give, "col", 1, n_col)
-    picked = picked + far
-    for group in ((1, 2, 3), (4,)):
-        parts = [swap(picked, "row", k, n_row) for k in group]
-        for part in parts:
-            picked = picked + part
-    joined = join(got, picked)
+    picked = add_up(picked, n_row)
+    joined = join(got, picked, keep.shape[1])
     near_rows, joined = lax.optimization_barrier((near_rows, joined))
     far_rows = to_chips(joined)
     other = swap(far_rows[:, keep.shape[1] :], "col", 1, n_col)
@@ -268,8 +281,9 @@
     share = pl.pallas_call(
         sum_kernel,
         out_shape=jax.ShapeDtypeStruct((n_row, evo, prows // n_row), F32),
-        in_specs=whole(1),
-        out_specs=whole(1)[0],
+        grid=(1,),
+        in_specs=[pl.BlockSpec((chips, evo, prows), lambda i: (0, 0, 0))],
+        out_specs=pl.BlockSpec((n_row, evo, prows // n_row), lambda i: (0, 0, 0)),
         cost_estimate=cost(home.size, 2 * home.size),
     )(home)
     share = lax.all_to_all(share, "row", 0, 0, tiled=True)
@@ -280,7 +294,7 @@
         in_specs=[pl.BlockSpec(memory_space=pltpu.SMEM)] + whole(2),
         out_specs=whole(1)[0],
         cost_estimate=cost(prior.size, 10 * prior.size),
-    )((me % 2).reshape(1), home, prior_t).T
+    )(core, home, prior_t).T
     return reobserved, projection
 
 

time: 129 us -> 125 us (0.969)
  blocking collectives: 56.6 us -> 52.6 us
  waiting for transfers between devices: 23.6 us -> 26.8 us
  Pallas kernels: 18.7 us -> 16.4 us
  starting transfers between devices: 27.8 us -> 25.7 us
    ppermute x0 -> x4, waiting for transfers between devices: none -> 12.5 us  [turn(): lax.ppermute(y, 'row', [(h * ring + z, h * ring + (z + by) % ring) for h...]
    ppermute x9 -> x5, starting transfers between devices: 13.4 us -> 3.68 us  [swap(): return lax.ppermute(x, axis, [(i, i ^ bits) for i in range(n)])]
    ppermute x0 -> x4, starting transfers between devices: none -> 7.24 us  [turn(): lax.ppermute(y, 'row', [(h * ring + z, h * ring + (z + by) % ring) for h...]
    ppermute x9 -> x5, waiting for transfers between devices: 14.4 us -> 7.2 us  [swap(): return lax.ppermute(x, axis, [(i, i ^ bits) for i in range(n)])]
    all_to_all x1, blocking collectives: 38.6 us -> 34.6 us  [on_device(): far_rows = to_chips(joined)]
    pallas_call x1, Pallas kernels: 3.86 us -> 1.7 us  [join(): pl.pallas_call(functools.partial(join_kernel, depth), out_shape=jax.Shape...]
    all_to_all x1, waiting for transfers between devices: 2.13 us -> 0.01 us  [on_device(): near_rows = to_chips(keep)]
  transfers between devices with their start and end apart: 11 -> 11, of which waited for: 7 -> 8; matrix products, arithmetic and copies ran while one was open for 1% -> 1% of each run, Pallas kernels for 8% -> 6%
where the time goes in v4:
time: 125 us; the launch traced here: 124 us
  blocking collectives  52.6 us (42%)
  waiting for transfers between devices  26.8 us (21%)
  starting transfers between devices  25.7 us (21%)
  Pallas kernels  16.4 us (13%)
  other arithmetic  2.13 us (2%)
    all_to_all x1, blocking collectives, on_device(): far_rows = to_chips(joined)  34.6 us
    all_to_all x1, blocking collectives, on_device(): home = to_chips(home)  18 us
    ppermute x4, waiting for transfers between devices, turn(): lax.ppermute(y, 'row', [(h * ring + z, h * ring + (z + by) % ring) for h...  12.5 us
    all_to_all x1, starting transfers between devices, on_device(): share = lax.all_to_all(share, 'row', 0, 0, tiled=True)  9.48 us
    ppermute x4, starting transfers between devices, turn(): lax.ppermute(y, 'row', [(h * ring + z, h * ring + (z + by) % ring) for h...  7.24 us
    ppermute x5, waiting for transfers between devices, swap(): return lax.ppermute(x, axis, [(i, i ^ bits) for i in range(n)])  7.2 us
    all_to_all x1, waiting for transfers between devices, on_device(): share = lax.all_to_all(share, 'row', 0, 0, tiled=True)  7.1 us
    all_to_all x1, starting transfers between devices, on_device(): near_rows = to_chips(keep)  5.31 us
  transfers between devices with their start and end apart: 11, of which 8 were waited for; matrix products, arithmetic and copies ran while one was open for 1% of the time, Pallas kernels for 6%

profile of v4, /device:TPU:32, one launch (start us, length us, event | category | flops | bytes accessed | tf_op | source)
XLA Modules:
  0.0 124.4 jit_solution(11301640470499828520)
XLA Ops:
  0.6 4.5 %shard_map.77 = (bf16[8,960,128]{2,1,0:T(8,128)(2,1)}, bf16[8,1216,128]{2,1,0:T(8,128)(2,1)}) custom-call(s32[1]{0:T(128)} %bitcast.core_ref, bf16[12288,128]{1,0:T(8,128)(2,1)} %obs_ref.1, f32[16,12288]{1,0:T(8,128)} %bitcast.10), custom_call_target="tpu_custom_call" | custom-call | bytes 7864320 | tf_op jit(solution)/shard_map/pallas_call | solution.py:47
  5.2 0.0 collective-permute-start
  5.2 5.3 %all-to-all-start = ((bf16[8,960,128]{2,1,0:T(8,128)(2,1)}), bf16[8,960,128]{2,1,0:T(8,128)(2,1)S(1)}, u32[]{:S(2)}, u32[]{:S(2)}) async-start(bf16[8,960,128]{2,1,0:T(8,128)(2,1)} %get-tuple-element.15), calls=%async_computation | async-start | bytes 3932160 | tf_op jit(solution)/shard_map/all_to_all | solution.py:258
  10.5 3.7 %shard_map.78 = bf16[16,2048]{1,0:T(8,128)(2,1)} custom-call(s32[1]{0:T(128)} %bitcast.3.first_ref, s32[1,2048]{1,0:T(1,128)} %bitcast.15, bf16[16,12288]{1,0:T(8,128)(2,1)} %bitcast.14), custom_call_target="tpu_custom_call" | custom-call | flops 805306368 | bytes 458752 | tf_op jit(solution)/shard_map/pallas_call | solution.py:114
  14.2 1.9 %collective-permute-start.2 = (bf16[16,2048]{1,0:T(8,128)(2,1)}, bf16[16,2048]{1,0:T(8,128)(2,1)S(1)}, u32[]{:S(2)}, u32[]{:S(2)}) collective-permute-start(bf16[16,2048]{1,0:T(8,128)(2,1)} %shard_map.78), channel_id=1, source_target_pairs={{0,16},{16,32},{32,48},{48,64},{64,80},{80,96},{96,112},{112,0},{1... | collective-permute-start | bytes 196616 | tf_op jit(solution)/shard_map/ppermute | solution.py:227
  16.1 0.1 collective-permute-start.1
  16.2 2.4 %collective-permute-done.2 = bf16[16,2048]{1,0:T(8,128)(2,1)S(1)} collective-permute-done((bf16[16,2048]{1,0:T(8,128)(2,1)}, bf16[16,2048]{1,0:T(8,128)(2,1)S(1)}, u32[]{:S(2)}, u32[]{:S(2)}) %collective-permute-start.2) | collective-permute-done | bytes 65568 | tf_op jit(solution)/shard_map/ppermute | solution.py:227
  18.7 1.9 %collective-permute-done.1 = bf16[16,2048]{1,0:T(8,128)(2,1)S(1)} collective-permute-done((bf16[16,2048]{1,0:T(8,128)(2,1)}, bf16[16,2048]{1,0:T(8,128)(2,1)S(1)}, u32[]{:S(2)}, u32[]{:S(2)}) %collective-permute-start.1) | collective-permute-done | bytes 65568 | tf_op jit(solution)/shard_map/ppermute | solution.py:227
  20.6 0.9 fusion
  21.4 5.2 %collective-permute-start.4 = (bf16[16,2048]{1,0:T(8,128)(2,1)S(1)}, bf16[16,2048]{1,0:T(8,128)(2,1)S(1)}, u32[]{:S(2)}, u32[]{:S(2)}) collective-permute-start(bf16[16,2048]{1,0:T(8,128)(2,1)S(1)} %get-tuple-element.25), channel_id=1, source_target_pairs={{0,48},{16,64},{32,80},{48,96},{64,112},{80,0},{96,16},{112,32},{1... | collective-permute-start | bytes 196616 | tf_op jit(solution)/shard_map/ppermute | solution.py:227
  26.6 4.5 %collective-permute-done.4 = bf16[16,2048]{1,0:T(8,128)(2,1)S(1)} collective-permute-done((bf16[16,2048]{1,0:T(8,128)(2,1)S(1)}, bf16[16,2048]{1,0:T(8,128)(2,1)S(1)}, u32[]{:S(2)}, u32[]{:S(2)}) %collective-permute-start.4) | collective-permute-done | bytes 65568 | tf_op jit(solution)/shard_map/ppermute | solution.py:227
  31.1 3.7 %collective-permute-done.3 = bf16[16,2048]{1,0:T(8,128)(2,1)S(1)} collective-permute-done((bf16[16,2048]{1,0:T(8,128)(2,1)S(1)}, bf16[16,2048]{1,0:T(8,128)(2,1)S(1)}, u32[]{:S(2)}, u32[]{:S(2)}) %collective-permute-start.3) | collective-permute-done | bytes 65568 | tf_op jit(solution)/shard_map/ppermute | solution.py:227
  34.8 3.0 %collective-permute-start.5 = (bf16[16,2048]{1,0:T(8,128)(2,1)S(1)}, bf16[16,2048]{1,0:T(8,128)(2,1)S(1)}, u32[]{:S(2)}, u32[]{:S(2)}) collective-permute-start(bf16[16,2048]{1,0:T(8,128)(2,1)S(1)} %add_add_fusion), channel_id=1, source_target_pairs={{0,128},{16,144},{32,160},{48,176},{64,192},{80,208},{96,224},{112... | collective-permute-start | bytes 196616 | tf_op jit(solution)/shard_map/ppermute | solution.py:239
  37.8 2.9 %collective-permute-done.5 = bf16[16,2048]{1,0:T(8,128)(2,1)S(1)} collective-permute-done((bf16[16,2048]{1,0:T(8,128)(2,1)S(1)}, bf16[16,2048]{1,0:T(8,128)(2,1)S(1)}, u32[]{:S(2)}, u32[]{:S(2)}) %collective-permute-start.5) | collective-permute-done | bytes 65568 | tf_op jit(solution)/shard_map/ppermute | solution.py:239
  40.7 0.6 add.24.picked_ref
  41.3 1.7 %shard_map.79 = bf16[8,1216,128]{2,1,0:T(8,128)(2,1)} custom-call(bf16[8,1216,128]{2,1,0:T(8,128)(2,1)} %collective-permute-done.got_ref, bf16[16,2048]{1,0:T(8,128)(2,1)} %add.24.picked_ref), custom_call_target="tpu_custom_call", output_to_operand_aliasing={{}: (0, {})} | custom-call | bytes 524288 | tf_op jit(solution)/shard_map/pallas_call | solution.py:80
  43.0 0.0 copy-start.1
  43.0 0.0 copy-start
  43.1 34.6 %all_to_all.20.far_ref = bf16[8,1216,128]{2,1,0:T(8,128)(2,1)S(1)} all-to-all(bf16[8,1216,128]{2,1,0:T(8,128)(2,1)} %shard_map.79), channel_id=1, replica_groups={{0,2,4,6,8,10,12,14},{1,3,5,7,9,11,13,15},{16,18,20,22,24,26,28,30},{17..., dimensions={0} | all-to-all | bytes 4980736 | tf_op jit(solution)/shard_map/all_to_all | solution.py:264
  77.7 0.1 collective-permute-start.6
  77.8 1.9 %collective-permute-done.6.other_ref = bf16[8,256,128]{2,1,0:T(8,128)(2,1)S(1)} collective-permute-done((bf16[8,256,128]{2,1,0:T(8,128)(2,1)S(1)}, bf16[8,256,128]{2,1,0:T(8,128)(2,1)S(1)}, u32[]{:S(2)}, u32[]{:S(2)}) %collective-permute-start.6) | collective-permute-done | bytes 524320 | tf_op jit(solution)/shard_map/ppermute | solution.py:239
  79.7 2.2 %shard_map.80 = (f32[8,16,2048]{2,1,0:T(8,128)S(1)}, f32[8,16,2048]{2,1,0:T(8,128)S(1)}, bf16[8,16,768]{2,1,0:T(8,128)(2,1)S(1)}, bf16[8,16,768]{2,1,0:T(8,128)(2,1)S(1)}) custom-call(s32[1]{0:T(128)} %bitcast.1.me_ref, bf16[8,960,128]{2,1,0:T(8,128)(2,1)S(1)} %all-to-all-done.near_ref, bf16[8,1216,128]{2,1,0:T(8,128)(2,1)S(1)} %all_to_all.20.far_ref, ...), custom_call_target="tpu_custom_call" | custom-call | flops 1610612736 | bytes 9175040 | tf_op jit(solution)/shard_map/pallas_call | solution.py:183
  81.9 0.2 collective-permute-start.7
  82.1 0.4 collective-permute-start.8
  82.5 2.4 %collective-permute-done.8.s_got = bf16[8,16,768]{2,1,0:T(8,128)(2,1)S(1)} collective-permute-done((bf16[8,16,768]{2,1,0:T(8,128)(2,1)S(1)}, bf16[8,16,768]{2,1,0:T(8,128)(2,1)S(1)}, u32[]{:S(2)}, u32[]{:S(2)}) %collective-permute-start.8) | collective-permute-done | bytes 196640 | tf_op jit(solution)/shard_map/ppermute | solution.py:239
  85.0 0.1 shard_map.81
  85.1 18.0 %all_to_all.21.msg_ref = bf16[8,16,3584]{2,1,0:T(8,128)(2,1)} all-to-all(bf16[8,16,3584]{2,1,0:T(8,128)(2,1)S(1)} %shard_map.81), channel_id=1, replica_groups={{0,2,4,6,8,10,12,14},{1,3,5,7,9,11,13,15},{16,18,20,22,24,26,28,30},{17..., dimensions={0} | all-to-all | bytes 1835008 | tf_op jit(solution)/shard_map/all_to_all | solution.py:280
  103.1 1.8 %shard_map.83 = f32[16,16,128]{2,1,0:T(8,128)} custom-call(bf16[8,16,3584]{2,1,0:T(8,128)(2,1)} %all_to_all.21.msg_ref), custom_call_target="tpu_custom_call" | custom-call | flops 458752 | bytes 917504 | tf_op jit(solution)/shard_map/pallas_call | solution.py:281
  104.8 9.5 %all-to-all-start.3 = ((f32[16,16,128]{2,1,0:T(8,128)}), f32[16,16,128]{2,1,0:T(8,128)S(1)}, u32[]{:S(2)}, u32[]{:S(2)}) async-start(f32[16,16,128]{2,1,0:T(8,128)} %shard_map.83), calls=%async_computation.3 | async-start | bytes 262144 | tf_op jit(solution)/shard_map/all_to_all | solution.py:289
  114.3 2.4 %shard_map.82 = f32[16,12288]{1,0:T(8,128)} custom-call(s32[1]{0:T(128)} %bitcast.core_ref, bf16[8,16,3584]{2,1,0:T(8,128)(2,1)} %all_to_all.21.msg_ref, f32[16,12288]{1,0:T(8,128)} %bitcast.11), custom_call_target="tpu_custom_call" | custom-call | flops 196608 | bytes 1966080 | tf_op jit(solution)/shard_map/pallas_call | solution.py:291
  116.7 7.1 %all-to-all-done.3 = f32[16,16,128]{2,1,0:T(8,128)S(1)} async-done(((f32[16,16,128]{2,1,0:T(8,128)}), f32[16,16,128]{2,1,0:T(8,128)S(1)}, u32[]{:S(2)}, u32[]{:S(2)}) %all-to-all-start.3) | async-done | bytes 131104 | tf_op jit(solution)/shard_map/all_to_all | solution.py:289
  123.8 0.6 reduce_sum.9
  (8 shorter events, 0.1 us)
Async XLA Ops:
  5.2 36.1 %collective-permute-start = (bf16[8,1216,128]{2,1,0:T(8,128)(2,1)}, bf16[8,1216,128]{2,1,0:T(8,128)(2,1)}, u32[]{:S(2)}, u32[]{:S(2)}) collective-permute-start(bf16[8,1216,128]{2,1,0:T(8,128)(2,1)} %get-tuple-element.16), channel_id=1, source_target_pairs={{0,1},{1,0},{2,3},{3,2},{4,5},{5,4},{6,7},{7,6},{8,9},{9,8},{10,11... | collective-permute-start | bytes 7471112 | tf_op jit(solution)/shard_map/ppermute | solution.py:239
  5.2 37.9 %all-to-all-start = ((bf16[8,960,128]{2,1,0:T(8,128)(2,1)}), bf16[8,960,128]{2,1,0:T(8,128)(2,1)S(1)}, u32[]{:S(2)}, u32[]{:S(2)}) async-start(bf16[8,960,128]{2,1,0:T(8,128)(2,1)} %get-tuple-element.15), calls=%async_computation | async-start | bytes 3932160 | tf_op jit(solution)/shard_map/all_to_all | solution.py:258
  14.2 4.5 %collective-permute-start.2 = (bf16[16,2048]{1,0:T(8,128)(2,1)}, bf16[16,2048]{1,0:T(8,128)(2,1)S(1)}, u32[]{:S(2)}, u32[]{:S(2)}) collective-permute-start(bf16[16,2048]{1,0:T(8,128)(2,1)} %shard_map.78), channel_id=1, source_target_pairs={{0,16},{16,32},{32,48},{48,64},{64,80},{80,96},{96,112},{112,0},{1... | collective-permute-start | bytes 196616 | tf_op jit(solution)/shard_map/ppermute | solution.py:227
  16.1 4.5 %collective-permute-start.1 = (bf16[16,2048]{1,0:T(8,128)(2,1)}, bf16[16,2048]{1,0:T(8,128)(2,1)S(1)}, u32[]{:S(2)}, u32[]{:S(2)}) collective-permute-start(bf16[16,2048]{1,0:T(8,128)(2,1)} %shard_map.78), channel_id=1, source_target_pairs={{0,112},{16,0},{32,16},{48,32},{64,48},{80,64},{96,80},{112,96},{1... | collective-permute-start | bytes 196616 | tf_op jit(solution)/shard_map/ppermute | solution.py:227
  21.4 9.7 %collective-permute-start.4 = (bf16[16,2048]{1,0:T(8,128)(2,1)S(1)}, bf16[16,2048]{1,0:T(8,128)(2,1)S(1)}, u32[]{:S(2)}, u32[]{:S(2)}) collective-permute-start(bf16[16,2048]{1,0:T(8,128)(2,1)S(1)} %get-tuple-element.25), channel_id=1, source_target_pairs={{0,48},{16,64},{32,80},{48,96},{64,112},{80,0},{96,16},{112,32},{1... | collective-permute-start | bytes 196616 | tf_op jit(solution)/shard_map/ppermute | solution.py:227
  26.6 8.1 %collective-permute-start.3 = (bf16[16,2048]{1,0:T(8,128)(2,1)S(1)}, bf16[16,2048]{1,0:T(8,128)(2,1)S(1)}, u32[]{:S(2)}, u32[]{:S(2)}) collective-permute-start(bf16[16,2048]{1,0:T(8,128)(2,1)S(1)} %get-tuple-element.24), channel_id=1, source_target_pairs={{0,80},{16,96},{32,112},{48,0},{64,16},{80,32},{96,48},{112,64},{1... | collective-permute-start | bytes 196616 | tf_op jit(solution)/shard_map/ppermute | solution.py:227
  34.8 5.9 %collective-permute-start.5 = (bf16[16,2048]{1,0:T(8,128)(2,1)S(1)}, bf16[16,2048]{1,0:T(8,128)(2,1)S(1)}, u32[]{:S(2)}, u32[]{:S(2)}) collective-permute-start(bf16[16,2048]{1,0:T(8,128)(2,1)S(1)} %add_add_fusion), channel_id=1, source_target_pairs={{0,128},{16,144},{32,160},{48,176},{64,192},{80,208},{96,224},{112... | collective-permute-start | bytes 196616 | tf_op jit(solution)/shard_map/ppermute | solution.py:239
  43.0 36.7 %copy-start.1 = (f32[12288]{0:T(1024)S(1)}, f32[12288]{0:T(1024)}, u32[]{:S(2)}) copy-start(f32[12288]{0:T(1024)} %param.10) | copy-start | bytes 147460
  43.0 36.7 %copy-start = (bf16[2048,768]{1,0:T(8,128)(2,1)S(1)}, bf16[2048,768]{1,0:T(8,128)(2,1)}, u32[]{:S(2)}) copy-start(bf16[2048,768]{1,0:T(8,128)(2,1)} %proj_ref.1) | copy-start | bytes 9437188
  77.7 2.0 %collective-permute-start.6 = (bf16[8,256,128]{2,1,0:T(8,128)(2,1)S(1)}, bf16[8,256,128]{2,1,0:T(8,128)(2,1)S(1)}, u32[]{:S(2)}, u32[]{:S(2)}) collective-permute-start(bf16[8,256,128]{2,1,0:T(8,128)(2,1)S(1)} %slice.4), channel_id=1, source_target_pairs={{0,1},{1,0},{2,3},{3,2},{4,5},{5,4},{6,7},{7,6},{8,9},{9,8},{10,11... | collective-permute-start | bytes 1572872 | tf_op jit(solution)/shard_map/ppermute | solution.py:239
  81.9 3.0 %collective-permute-start.7 = (f32[8,16,2048]{2,1,0:T(8,128)S(1)}, f32[8,16,2048]{2,1,0:T(8,128)S(1)}, u32[]{:S(2)}, u32[]{:S(2)}) collective-permute-start(f32[8,16,2048]{2,1,0:T(8,128)S(1)} %get-tuple-element.21), channel_id=1, source_target_pairs={{0,1},{1,0},{2,3},{3,2},{4,5},{5,4},{6,7},{7,6},{8,9},{9,8},{10,11... | collective-permute-start | bytes 3145736 | tf_op jit(solution)/shard_map/ppermute | solution.py:239
  82.1 2.8 %collective-permute-start.8 = (bf16[8,16,768]{2,1,0:T(8,128)(2,1)S(1)}, bf16[8,16,768]{2,1,0:T(8,128)(2,1)S(1)}, u32[]{:S(2)}, u32[]{:S(2)}) collective-permute-start(bf16[8,16,768]{2,1,0:T(8,128)(2,1)S(1)} %get-tuple-element.23), channel_id=1, source_target_pairs={{0,1},{1,0},{2,3},{3,2},{4,5},{5,4},{6,7},{7,6},{8,9},{9,8},{10,11... | collective-permute-start | bytes 589832 | tf_op jit(solution)/shard_map/ppermute | solution.py:239
  104.8 18.9 %all-to-all-start.3 = ((f32[16,16,128]{2,1,0:T(8,128)}), f32[16,16,128]{2,1,0:T(8,128)S(1)}, u32[]{:S(2)}, u32[]{:S(2)}) async-start(f32[16,16,128]{2,1,0:T(8,128)} %shard_map.83), calls=%async_computation.3 | async-start | bytes 262144 | tf_op jit(solution)/shard_map/all_to_all | solution.py:289

commit v5 on v4

--- a/solution.py
+++ b/solution.py
@@ -42,7 +42,7 @@
     evo = prior_t.shape[0]
     sub = rows // n_col
     depth = sub + 2 * evo * sub // LANES
-    chips = 2
+    chips = 4
     block = pl.BlockSpec((chips, depth, width), lambda i, _: (i, 0, 0))
     return pl.pallas_call(
         functools.partial(pack_kernel, chips),
@@ -110,7 +110,7 @@
 def pick(first, idx, sky):
     evo, rows = sky.shape
     count = idx.shape[1]
-    tile = 512
+    tile = 1024
     return pl.pallas_call(
         pick_kernel,
         out_shape=jax.ShapeDtypeStruct((evo, count), BF16),

time: 125 us -> 124 us (level)
  Pallas kernels: 16.4 us -> 14.7 us
where the time goes in v5:
time: 124 us; the launch traced here: 123 us
  blocking collectives  52.6 us (42%)
  waiting for transfers between devices  26.8 us (22%)
  starting transfers between devices  26.4 us (21%)
  Pallas kernels  14.7 us (12%)
  other arithmetic  2.13 us (2%)
    all_to_all x1, blocking collectives, on_device(): far_rows = to_chips(joined)  34.6 us
    all_to_all x1, blocking collectives, on_device(): home = to_chips(home)  18 us
    ppermute x4, waiting for transfers between devices, turn(): lax.ppermute(y, 'row', [(h * ring + z, h * ring + (z + by) % ring) for h...  12.5 us
    all_to_all x1, starting transfers between devices, on_device(): share = lax.all_to_all(share, 'row', 0, 0, tiled=True)  10.2 us
    ppermute x4, starting transfers between devices, turn(): lax.ppermute(y, 'row', [(h * ring + z, h * ring + (z + by) % ring) for h...  7.24 us
    ppermute x5, waiting for transfers between devices, swap(): return lax.ppermute(x, axis, [(i, i ^ bits) for i in range(n)])  7.2 us
    all_to_all x1, waiting for transfers between devices, on_device(): share = lax.all_to_all(share, 'row', 0, 0, tiled=True)  7.1 us
    all_to_all x1, starting transfers between devices, on_device(): near_rows = to_chips(keep)  5.31 us
  transfers between devices with their start and end apart: 11, of which 8 were waited for; matrix products, arithmetic and copies ran while one was open for 1% of the time, Pallas kernels for 6%

profile of v5, /device:TPU:32, one launch (start us, length us, event | category | flops | bytes accessed | tf_op | source)
XLA Modules:
  0.0 123.4 jit_solution(12517271185320486708)
XLA Ops:
  0.6 3.5 %shard_map.77 = (bf16[8,960,128]{2,1,0:T(8,128)(2,1)}, bf16[8,1216,128]{2,1,0:T(8,128)(2,1)}) custom-call(s32[1]{0:T(128)} %bitcast.core_ref, bf16[12288,128]{1,0:T(8,128)(2,1)} %obs_ref.1, f32[16,12288]{1,0:T(8,128)} %bitcast.10), custom_call_target="tpu_custom_call" | custom-call | bytes 7864320 | tf_op jit(solution)/shard_map/pallas_call | solution.py:47
  4.1 0.0 collective-permute-start
  4.1 5.3 %all-to-all-start = ((bf16[8,960,128]{2,1,0:T(8,128)(2,1)}), bf16[8,960,128]{2,1,0:T(8,128)(2,1)S(1)}, u32[]{:S(2)}, u32[]{:S(2)}) async-start(bf16[8,960,128]{2,1,0:T(8,128)(2,1)} %get-tuple-element.15), calls=%async_computation | async-start | bytes 3932160 | tf_op jit(solution)/shard_map/all_to_all | solution.py:258
  9.5 3.0 %shard_map.78 = bf16[16,2048]{1,0:T(8,128)(2,1)} custom-call(s32[1]{0:T(128)} %bitcast.3.first_ref, s32[1,2048]{1,0:T(1,128)} %bitcast.15, bf16[16,12288]{1,0:T(8,128)(2,1)} %bitcast.14), custom_call_target="tpu_custom_call" | custom-call | flops 805306368 | bytes 458752 | tf_op jit(solution)/shard_map/pallas_call | solution.py:114
  12.4 1.9 %collective-permute-start.2 = (bf16[16,2048]{1,0:T(8,128)(2,1)}, bf16[16,2048]{1,0:T(8,128)(2,1)S(1)}, u32[]{:S(2)}, u32[]{:S(2)}) collective-permute-start(bf16[16,2048]{1,0:T(8,128)(2,1)} %shard_map.78), channel_id=1, source_target_pairs={{0,16},{16,32},{32,48},{48,64},{64,80},{80,96},{96,112},{112,0},{1... | collective-permute-start | bytes 196616 | tf_op jit(solution)/shard_map/ppermute | solution.py:227
  14.4 0.1 collective-permute-start.1
  14.5 2.4 %collective-permute-done.2 = bf16[16,2048]{1,0:T(8,128)(2,1)S(1)} collective-permute-done((bf16[16,2048]{1,0:T(8,128)(2,1)}, bf16[16,2048]{1,0:T(8,128)(2,1)S(1)}, u32[]{:S(2)}, u32[]{:S(2)}) %collective-permute-start.2) | collective-permute-done | bytes 65568 | tf_op jit(solution)/shard_map/ppermute | solution.py:227
  16.9 1.9 %collective-permute-done.1 = bf16[16,2048]{1,0:T(8,128)(2,1)S(1)} collective-permute-done((bf16[16,2048]{1,0:T(8,128)(2,1)}, bf16[16,2048]{1,0:T(8,128)(2,1)S(1)}, u32[]{:S(2)}, u32[]{:S(2)}) %collective-permute-start.1) | collective-permute-done | bytes 65568 | tf_op jit(solution)/shard_map/ppermute | solution.py:227
  18.8 0.9 fusion
  19.7 5.2 %collective-permute-start.4 = (bf16[16,2048]{1,0:T(8,128)(2,1)S(1)}, bf16[16,2048]{1,0:T(8,128)(2,1)S(1)}, u32[]{:S(2)}, u32[]{:S(2)}) collective-permute-start(bf16[16,2048]{1,0:T(8,128)(2,1)S(1)} %get-tuple-element.25), channel_id=1, source_target_pairs={{0,48},{16,64},{32,80},{48,96},{64,112},{80,0},{96,16},{112,32},{1... | collective-permute-start | bytes 196616 | tf_op jit(solution)/shard_map/ppermute | solution.py:227
  24.9 4.5 %collective-permute-done.4 = bf16[16,2048]{1,0:T(8,128)(2,1)S(1)} collective-permute-done((bf16[16,2048]{1,0:T(8,128)(2,1)S(1)}, bf16[16,2048]{1,0:T(8,128)(2,1)S(1)}, u32[]{:S(2)}, u32[]{:S(2)}) %collective-permute-start.4) | collective-permute-done | bytes 65568 | tf_op jit(solution)/shard_map/ppermute | solution.py:227
  29.4 3.7 %collective-permute-done.3 = bf16[16,2048]{1,0:T(8,128)(2,1)S(1)} collective-permute-done((bf16[16,2048]{1,0:T(8,128)(2,1)S(1)}, bf16[16,2048]{1,0:T(8,128)(2,1)S(1)}, u32[]{:S(2)}, u32[]{:S(2)}) %collective-permute-start.3) | collective-permute-done | bytes 65568 | tf_op jit(solution)/shard_map/ppermute | solution.py:227
  33.1 3.0 %collective-permute-start.5 = (bf16[16,2048]{1,0:T(8,128)(2,1)S(1)}, bf16[16,2048]{1,0:T(8,128)(2,1)S(1)}, u32[]{:S(2)}, u32[]{:S(2)}) collective-permute-start(bf16[16,2048]{1,0:T(8,128)(2,1)S(1)} %add_add_fusion), channel_id=1, source_target_pairs={{0,128},{16,144},{32,160},{48,176},{64,192},{80,208},{96,224},{112... | collective-permute-start | bytes 196616 | tf_op jit(solution)/shard_map/ppermute | solution.py:239
  36.0 2.9 %collective-permute-done.5 = bf16[16,2048]{1,0:T(8,128)(2,1)S(1)} collective-permute-done((bf16[16,2048]{1,0:T(8,128)(2,1)S(1)}, bf16[16,2048]{1,0:T(8,128)(2,1)S(1)}, u32[]{:S(2)}, u32[]{:S(2)}) %collective-permute-start.5) | collective-permute-done | bytes 65568 | tf_op jit(solution)/shard_map/ppermute | solution.py:239
  38.9 0.6 add.24.picked_ref
  39.6 1.7 %shard_map.79 = bf16[8,1216,128]{2,1,0:T(8,128)(2,1)} custom-call(bf16[8,1216,128]{2,1,0:T(8,128)(2,1)} %collective-permute-done.got_ref, bf16[16,2048]{1,0:T(8,128)(2,1)} %add.24.picked_ref), custom_call_target="tpu_custom_call", output_to_operand_aliasing={{}: (0, {})} | custom-call | bytes 524288 | tf_op jit(solution)/shard_map/pallas_call | solution.py:80
  41.3 0.0 copy-start.1
  41.3 0.0 copy-start
  41.3 34.6 %all_to_all.20.far_ref = bf16[8,1216,128]{2,1,0:T(8,128)(2,1)S(1)} all-to-all(bf16[8,1216,128]{2,1,0:T(8,128)(2,1)} %shard_map.79), channel_id=1, replica_groups={{0,2,4,6,8,10,12,14},{1,3,5,7,9,11,13,15},{16,18,20,22,24,26,28,30},{17..., dimensions={0} | all-to-all | bytes 4980736 | tf_op jit(solution)/shard_map/all_to_all | solution.py:264
  76.0 0.1 collective-permute-start.6
  76.1 1.9 %collective-permute-done.6.other_ref = bf16[8,256,128]{2,1,0:T(8,128)(2,1)S(1)} collective-permute-done((bf16[8,256,128]{2,1,0:T(8,128)(2,1)S(1)}, bf16[8,256,128]{2,1,0:T(8,128)(2,1)S(1)}, u32[]{:S(2)}, u32[]{:S(2)}) %collective-permute-start.6) | collective-permute-done | bytes 524320 | tf_op jit(solution)/shard_map/ppermute | solution.py:239
  78.0 2.2 %shard_map.80 = (f32[8,16,2048]{2,1,0:T(8,128)S(1)}, f32[8,16,2048]{2,1,0:T(8,128)S(1)}, bf16[8,16,768]{2,1,0:T(8,128)(2,1)S(1)}, bf16[8,16,768]{2,1,0:T(8,128)(2,1)S(1)}) custom-call(s32[1]{0:T(128)} %bitcast.1.me_ref, bf16[8,960,128]{2,1,0:T(8,128)(2,1)S(1)} %all-to-all-done.near_ref, bf16[8,1216,128]{2,1,0:T(8,128)(2,1)S(1)} %all_to_all.20.far_ref, ...), custom_call_target="tpu_custom_call" | custom-call | flops 1610612736 | bytes 9175040 | tf_op jit(solution)/shard_map/pallas_call | solution.py:183
  80.2 0.2 collective-permute-start.7
  80.4 0.4 collective-permute-start.8
  80.8 2.4 %collective-permute-done.8.s_got = bf16[8,16,768]{2,1,0:T(8,128)(2,1)S(1)} collective-permute-done((bf16[8,16,768]{2,1,0:T(8,128)(2,1)S(1)}, bf16[8,16,768]{2,1,0:T(8,128)(2,1)S(1)}, u32[]{:S(2)}, u32[]{:S(2)}) %collective-permute-start.8) | collective-permute-done | bytes 196640 | tf_op jit(solution)/shard_map/ppermute | solution.py:239
  83.2 0.1 shard_map.81
  83.3 18.0 %all_to_all.21.msg_ref = bf16[8,16,3584]{2,1,0:T(8,128)(2,1)} all-to-all(bf16[8,16,3584]{2,1,0:T(8,128)(2,1)S(1)} %shard_map.81), channel_id=1, replica_groups={{0,2,4,6,8,10,12,14},{1,3,5,7,9,11,13,15},{16,18,20,22,24,26,28,30},{17..., dimensions={0} | all-to-all | bytes 1835008 | tf_op jit(solution)/shard_map/all_to_all | solution.py:280
  101.3 1.8 %shard_map.83 = f32[16,16,128]{2,1,0:T(8,128)} custom-call(bf16[8,16,3584]{2,1,0:T(8,128)(2,1)} %all_to_all.21.msg_ref), custom_call_target="tpu_custom_call" | custom-call | flops 458752 | bytes 917504 | tf_op jit(solution)/shard_map/pallas_call | solution.py:281
  103.1 10.2 %all-to-all-start.3 = ((f32[16,16,128]{2,1,0:T(8,128)}), f32[16,16,128]{2,1,0:T(8,128)S(1)}, u32[]{:S(2)}, u32[]{:S(2)}) async-start(f32[16,16,128]{2,1,0:T(8,128)} %shard_map.83), calls=%async_computation.3 | async-start | bytes 262144 | tf_op jit(solution)/shard_map/all_to_all | solution.py:289
  113.3 2.4 %shard_map.82 = f32[16,12288]{1,0:T(8,128)} custom-call(s32[1]{0:T(128)} %bitcast.core_ref, bf16[8,16,3584]{2,1,0:T(8,128)(2,1)} %all_to_all.21.msg_ref, f32[16,12288]{1,0:T(8,128)} %bitcast.11), custom_call_target="tpu_custom_call" | custom-call | flops 196608 | bytes 1966080 | tf_op jit(solution)/shard_map/pallas_call | solution.py:291
  115.6 7.1 %all-to-all-done.3 = f32[16,16,128]{2,1,0:T(8,128)S(1)} async-done(((f32[16,16,128]{2,1,0:T(8,128)}), f32[16,16,128]{2,1,0:T(8,128)S(1)}, u32[]{:S(2)}, u32[]{:S(2)}) %all-to-all-start.3) | async-done | bytes 131104 | tf_op jit(solution)/shard_map/all_to_all | solution.py:289
  122.7 0.6 reduce_sum.9
  (8 shorter events, 0.1 us)
Async XLA Ops:
  4.1 35.4 %collective-permute-start = (bf16[8,1216,128]{2,1,0:T(8,128)(2,1)}, bf16[8,1216,128]{2,1,0:T(8,128)(2,1)}, u32[]{:S(2)}, u32[]{:S(2)}) collective-permute-start(bf16[8,1216,128]{2,1,0:T(8,128)(2,1)} %get-tuple-element.16), channel_id=1, source_target_pairs={{0,1},{1,0},{2,3},{3,2},{4,5},{5,4},{6,7},{7,6},{8,9},{9,8},{10,11... | collective-permute-start | bytes 7471112 | tf_op jit(solution)/shard_map/ppermute | solution.py:239
  4.1 37.2 %all-to-all-start = ((bf16[8,960,128]{2,1,0:T(8,128)(2,1)}), bf16[8,960,128]{2,1,0:T(8,128)(2,1)S(1)}, u32[]{:S(2)}, u32[]{:S(2)}) async-start(bf16[8,960,128]{2,1,0:T(8,128)(2,1)} %get-tuple-element.15), calls=%async_computation | async-start | bytes 3932160 | tf_op jit(solution)/shard_map/all_to_all | solution.py:258
  12.4 4.5 %collective-permute-start.2 = (bf16[16,2048]{1,0:T(8,128)(2,1)}, bf16[16,2048]{1,0:T(8,128)(2,1)S(1)}, u32[]{:S(2)}, u32[]{:S(2)}) collective-permute-start(bf16[16,2048]{1,0:T(8,128)(2,1)} %shard_map.78), channel_id=1, source_target_pairs={{0,16},{16,32},{32,48},{48,64},{64,80},{80,96},{96,112},{112,0},{1... | collective-permute-start | bytes 196616 | tf_op jit(solution)/shard_map/ppermute | solution.py:227
  14.4 4.5 %collective-permute-start.1 = (bf16[16,2048]{1,0:T(8,128)(2,1)}, bf16[16,2048]{1,0:T(8,128)(2,1)S(1)}, u32[]{:S(2)}, u32[]{:S(2)}) collective-permute-start(bf16[16,2048]{1,0:T(8,128)(2,1)} %shard_map.78), channel_id=1, source_target_pairs={{0,112},{16,0},{32,16},{48,32},{64,48},{80,64},{96,80},{112,96},{1... | collective-permute-start | bytes 196616 | tf_op jit(solution)/shard_map/ppermute | solution.py:227
  19.7 9.7 %collective-permute-start.4 = (bf16[16,2048]{1,0:T(8,128)(2,1)S(1)}, bf16[16,2048]{1,0:T(8,128)(2,1)S(1)}, u32[]{:S(2)}, u32[]{:S(2)}) collective-permute-start(bf16[16,2048]{1,0:T(8,128)(2,1)S(1)} %get-tuple-element.25), channel_id=1, source_target_pairs={{0,48},{16,64},{32,80},{48,96},{64,112},{80,0},{96,16},{112,32},{1... | collective-permute-start | bytes 196616 | tf_op jit(solution)/shard_map/ppermute | solution.py:227
  24.9 8.1 %collective-permute-start.3 = (bf16[16,2048]{1,0:T(8,128)(2,1)S(1)}, bf16[16,2048]{1,0:T(8,128)(2,1)S(1)}, u32[]{:S(2)}, u32[]{:S(2)}) collective-permute-start(bf16[16,2048]{1,0:T(8,128)(2,1)S(1)} %get-tuple-element.24), channel_id=1, source_target_pairs={{0,80},{16,96},{32,112},{48,0},{64,16},{80,32},{96,48},{112,64},{1... | collective-permute-start | bytes 196616 | tf_op jit(solution)/shard_map/ppermute | solution.py:227
  33.1 5.9 %collective-permute-start.5 = (bf16[16,2048]{1,0:T(8,128)(2,1)S(1)}, bf16[16,2048]{1,0:T(8,128)(2,1)S(1)}, u32[]{:S(2)}, u32[]{:S(2)}) collective-permute-start(bf16[16,2048]{1,0:T(8,128)(2,1)S(1)} %add_add_fusion), channel_id=1, source_target_pairs={{0,128},{16,144},{32,160},{48,176},{64,192},{80,208},{96,224},{112... | collective-permute-start | bytes 196616 | tf_op jit(solution)/shard_map/ppermute | solution.py:239
  41.3 36.7 %copy-start.1 = (f32[12288]{0:T(1024)S(1)}, f32[12288]{0:T(1024)}, u32[]{:S(2)}) copy-start(f32[12288]{0:T(1024)} %param.10) | copy-start | bytes 147460
  41.3 36.7 %copy-start = (bf16[2048,768]{1,0:T(8,128)(2,1)S(1)}, bf16[2048,768]{1,0:T(8,128)(2,1)}, u32[]{:S(2)}) copy-start(bf16[2048,768]{1,0:T(8,128)(2,1)} %proj_ref.1) | copy-start | bytes 9437188
  76.0 2.0 %collective-permute-start.6 = (bf16[8,256,128]{2,1,0:T(8,128)(2,1)S(1)}, bf16[8,256,128]{2,1,0:T(8,128)(2,1)S(1)}, u32[]{:S(2)}, u32[]{:S(2)}) collective-permute-start(bf16[8,256,128]{2,1,0:T(8,128)(2,1)S(1)} %slice.4), channel_id=1, source_target_pairs={{0,1},{1,0},{2,3},{3,2},{4,5},{5,4},{6,7},{7,6},{8,9},{9,8},{10,11... | collective-permute-start | bytes 1572872 | tf_op jit(solution)/shard_map/ppermute | solution.py:239
  80.2 3.0 %collective-permute-start.7 = (f32[8,16,2048]{2,1,0:T(8,128)S(1)}, f32[8,16,2048]{2,1,0:T(8,128)S(1)}, u32[]{:S(2)}, u32[]{:S(2)}) collective-permute-start(f32[8,16,2048]{2,1,0:T(8,128)S(1)} %get-tuple-element.21), channel_id=1, source_target_pairs={{0,1},{1,0},{2,3},{3,2},{4,5},{5,4},{6,7},{7,6},{8,9},{9,8},{10,11... | collective-permute-start | bytes 3145736 | tf_op jit(solution)/shard_map/ppermute | solution.py:239
  80.4 2.8 %collective-permute-start.8 = (bf16[8,16,768]{2,1,0:T(8,128)(2,1)S(1)}, bf16[8,16,768]{2,1,0:T(8,128)(2,1)S(1)}, u32[]{:S(2)}, u32[]{:S(2)}) collective-permute-start(bf16[8,16,768]{2,1,0:T(8,128)(2,1)S(1)} %get-tuple-element.23), channel_id=1, source_target_pairs={{0,1},{1,0},{2,3},{3,2},{4,5},{5,4},{6,7},{7,6},{8,9},{9,8},{10,11... | collective-permute-start | bytes 589832 | tf_op jit(solution)/shard_map/ppermute | solution.py:239
  103.1 19.6 %all-to-all-start.3 = ((f32[16,16,128]{2,1,0:T(8,128)}), f32[16,16,128]{2,1,0:T(8,128)S(1)}, u32[]{:S(2)}, u32[]{:S(2)}) async-start(f32[16,16,128]{2,1,0:T(8,128)} %shard_map.83), calls=%async_computation.3 | async-start | bytes 262144 | tf_op jit(solution)/shard_map/all_to_all | solution.py:289

commit v6 on v5

--- a/solution.py
+++ b/solution.py
@@ -128,40 +128,34 @@
 
 
 def main_kernel(
-    me_ref, near_ref, far_ref, other_ref, apod_ref, proj_ref, p_own, p_other, s_own, s_other, panel, weighted
+    at_pick, me_ref, near_ref, far_ref, pick_ref, prior_ref, apod_ref, proj_ref, p_ref, s_ref, panel, weighted
 ):
-    chips, evo, _ = p_own.shape
+    chips, evo, _ = p_ref.shape
     prows, sub = proj_ref.shape
     me = me_ref[0]
     core = me % 2
     half = chips * evo
-    depth = near_ref.shape[1]
     for k in range(chips):
         for side in range(2):
-            tile = (2 * k + jnp.bitwise_xor(core, side)) * evo
+            tile = pl.ds(pl.multiple_of(at_pick + (2 * k + jnp.bitwise_xor(core, side)) * evo, evo), evo)
             lanes = slice((2 * k + side) * LANES, (2 * k + side + 1) * LANES)
             for m in range(chips):
-                panel[m * evo : (m + 1) * evo, lanes] = far_ref[m, pl.ds(pl.multiple_of(depth + tile, evo), evo)]
-                panel[half + m * evo : half + (m + 1) * evo, lanes] = other_ref[
-                    m, pl.ds(pl.multiple_of(tile, evo), evo)
-                ]
+                panel[m * evo : (m + 1) * evo, lanes] = pick_ref[m, tile]
     for n in range(sub // WIDE):
         rows = slice(n * WIDE, (n + 1) * WIDE)
-        added = jnp.zeros((2 * half, WIDE), F32)
+        added = jnp.zeros((half, WIDE), F32)
         for k in range(chips):
             obs = jnp.concatenate([near_ref[k, rows], far_ref[k, rows]], axis=1)
             added += lax.dot_general(
                 panel[:, k * WIDE : (k + 1) * WIDE], obs, NT, preferred_element_type=F32
             )
-        s_own[:, :, rows] = added[:half].astype(BF16).reshape(chips, evo, WIDE)
-        s_other[:, :, rows] = added[half:].astype(BF16).reshape(chips, evo, WIDE)
+        s_ref[:, :, rows] = added.astype(BF16).reshape(chips, evo, WIDE)
         for l in range(WIDE // LANES):
             block = n * (WIDE // LANES) + l
             row = sub + block * 2 * evo
             prior = jnp.concatenate(
                 [
-                    ref[m, row : row + evo].astype(F32) + ref[m, row + evo : row + 2 * evo].astype(F32)
-                    for ref in (near_ref, far_ref)
+                    prior_ref[m, row : row + evo].astype(F32) + prior_ref[m, row + evo : row + 2 * evo].astype(F32)
                     for m in range(chips)
                 ],
                 axis=0,
@@ -172,28 +166,25 @@
     for n in range(prows // WIDE):
         cols = slice(n * WIDE, (n + 1) * WIDE)
         part = lax.dot_general(weighted[...], proj_ref[cols], NT, preferred_element_type=F32)
-        p_own[:, :, cols] = part[:half].reshape(chips, evo, WIDE)
-        p_other[:, :, cols] = part[half:].reshape(chips, evo, WIDE)
-
-
-def main_step(me, near, far, other, apod, proj, evo, count):
+        p_ref[:, :, cols] = part.reshape(chips, evo, WIDE)
+
+
+def main_step(at_pick, me, near, far, picks, prior, apod, proj, evo, count):
     chips = near.shape[0]
     prows, sub = proj.shape
-    total = 2 * chips * evo
+    total = chips * evo
     return pl.pallas_call(
-        main_kernel,
+        functools.partial(main_kernel, at_pick),
         out_shape=(
             jax.ShapeDtypeStruct((chips, evo, prows), F32),
-            jax.ShapeDtypeStruct((chips, evo, prows), F32),
-            jax.ShapeDtypeStruct((chips, evo, sub), BF16),
             jax.ShapeDtypeStruct((chips, evo, sub), BF16),
         ),
-        in_specs=[pl.BlockSpec(memory_space=pltpu.SMEM)] + whole(5),
-        out_specs=tuple(whole(4)),
+        in_specs=[pl.BlockSpec(memory_space=pltpu.SMEM)] + whole(6),
+        out_specs=tuple(whole(2)),
         scratch_shapes=[pltpu.VMEM((total, count), BF16), pltpu.VMEM((total, sub), BF16)],
         compiler_params=pltpu.CompilerParams(vmem_limit_bytes=28 * MIB),
         cost_estimate=cost(2 * total * sub * (count + prows), 4 * near.size + 2 * proj.size + 4 * total * prows),
-    )(me, near, far, other, apod, proj)
+    )(me, near, far, picks, prior, apod, proj)
 
 
 def home_kernel(p_own, p_got, s_own, s_got, out_ref):
@@ -264,9 +255,10 @@
     far_rows = to_chips(joined)
     other = swap(far_rows[:, keep.shape[1] :], "col", 1, n_col)
 
-    p_own, p_other, s_own, s_other = main_step(
-        me.reshape(1), near_rows, far_rows, other, apod.reshape(rows_blk // LANES, LANES), proj, evo, count
-    )
+    weights = apod.reshape(rows_blk // LANES, LANES)
+    rest = (weights, proj, evo, count)
+    p_own, s_own = main_step(keep.shape[1], me.reshape(1), near_rows, far_rows, far_rows, near_rows, *rest)
+    p_other, s_other = main_step(0, me.reshape(1), near_rows, far_rows, other, far_rows, *rest)
     p_got = swap(p_other, "col", 1, n_col)
     s_got = swap(s_other, "col", 1, n_col)
     home = pl.pallas_call(

time: 124 us -> 124 us (level)
  Pallas kernels: 14.7 us -> 17.2 us
  waiting for transfers between devices: 26.8 us -> 24.4 us
    pallas_call x1 -> x2, Pallas kernels: 2.22 us -> 4.76 us  [main_step(): pl.pallas_call(functools.partial(main_kernel, at_pick), out_shape=(jax.Sh...]
    ppermute x5, waiting for transfers between devices: 7.2 us -> 4.82 us  [swap(): return lax.ppermute(x, axis, [(i, i ^ bits) for i in range(n)])]
  transfers between devices with their start and end apart: 11 -> 11, of which waited for: 8 -> 7; matrix products, arithmetic and copies ran while one was open for 1% -> 1% of each run, Pallas kernels for 6% -> 8%
where the time goes in v6:
time: 124 us
  blocking collectives  52.6 us (42%)
  starting transfers between devices  26.4 us (21%)
  waiting for transfers between devices  24.4 us (20%)
  Pallas kernels  17.2 us (14%)
  other arithmetic  2.13 us (2%)
    all_to_all x1, blocking collectives, on_device(): far_rows = to_chips(joined)  34.6 us
    all_to_all x1, blocking collectives, on_device(): home = to_chips(home)  18 us
    ppermute x4, waiting for transfers between devices, turn(): lax.ppermute(y, 'row', [(h * ring + z, h * ring + (z + by) % ring) for h...  12.5 us
    all_to_all x1, starting transfers between devices, on_device(): share = lax.all_to_all(share, 'row', 0, 0, tiled=True)  10.2 us
    ppermute x4, starting transfers between devices, turn(): lax.ppermute(y, 'row', [(h * ring + z, h * ring + (z + by) % ring) for h...  7.24 us
    all_to_all x1, waiting for transfers between devices, on_device(): share = lax.all_to_all(share, 'row', 0, 0, tiled=True)  7.1 us
    all_to_all x1, starting transfers between devices, on_device(): near_rows = to_chips(keep)  5.31 us
    ppermute x5, waiting for transfers between devices, swap(): return lax.ppermute(x, axis, [(i, i ^ bits) for i in range(n)])  4.82 us
  transfers between devices with their start and end apart: 11, of which 7 were waited for; matrix products, arithmetic and copies ran while one was open for 1% of the time, Pallas kernels for 8%

profile of v6, /device:TPU:32, one launch (start us, length us, event | category | flops | bytes accessed | tf_op | source)
XLA Modules:
  0.0 123.6 jit_solution(3783918101201373314)
XLA Ops:
  0.6 3.5 %shard_map.77 = (bf16[8,960,128]{2,1,0:T(8,128)(2,1)}, bf16[8,1216,128]{2,1,0:T(8,128)(2,1)}) custom-call(s32[1]{0:T(128)} %bitcast.core_ref, bf16[12288,128]{1,0:T(8,128)(2,1)} %obs_ref.1, f32[16,12288]{1,0:T(8,128)} %bitcast.11), custom_call_target="tpu_custom_call" | custom-call | bytes 7864320 | tf_op jit(solution)/shard_map/pallas_call | solution.py:47
  4.2 5.3 %all-to-all-start = ((bf16[8,960,128]{2,1,0:T(8,128)(2,1)}), bf16[8,960,128]{2,1,0:T(8,128)(2,1)S(1)}, u32[]{:S(2)}, u32[]{:S(2)}) async-start(bf16[8,960,128]{2,1,0:T(8,128)(2,1)} %get-tuple-element.15), calls=%async_computation | async-start | bytes 3932160 | tf_op jit(solution)/shard_map/all_to_all | solution.py:249
  9.5 3.0 %shard_map.78 = bf16[16,2048]{1,0:T(8,128)(2,1)} custom-call(s32[1]{0:T(128)} %bitcast.3.first_ref, s32[1,2048]{1,0:T(1,128)} %bitcast.16, bf16[16,12288]{1,0:T(8,128)(2,1)} %bitcast.15), custom_call_target="tpu_custom_call" | custom-call | flops 805306368 | bytes 458752 | tf_op jit(solution)/shard_map/pallas_call | solution.py:114
  12.5 1.9 %collective-permute-start.2 = (bf16[16,2048]{1,0:T(8,128)(2,1)}, bf16[16,2048]{1,0:T(8,128)(2,1)S(1)}, u32[]{:S(2)}, u32[]{:S(2)}) collective-permute-start(bf16[16,2048]{1,0:T(8,128)(2,1)} %shard_map.78), channel_id=1, source_target_pairs={{0,16},{16,32},{32,48},{48,64},{64,80},{80,96},{96,112},{112,0},{1... | collective-permute-start | bytes 196616 | tf_op jit(solution)/shard_map/ppermute | solution.py:218
  14.4 0.1 collective-permute-start.1
  14.5 2.4 %collective-permute-done.2 = bf16[16,2048]{1,0:T(8,128)(2,1)S(1)} collective-permute-done((bf16[16,2048]{1,0:T(8,128)(2,1)}, bf16[16,2048]{1,0:T(8,128)(2,1)S(1)}, u32[]{:S(2)}, u32[]{:S(2)}) %collective-permute-start.2) | collective-permute-done | bytes 65568 | tf_op jit(solution)/shard_map/ppermute | solution.py:218
  17.0 1.9 %collective-permute-done.1 = bf16[16,2048]{1,0:T(8,128)(2,1)S(1)} collective-permute-done((bf16[16,2048]{1,0:T(8,128)(2,1)}, bf16[16,2048]{1,0:T(8,128)(2,1)S(1)}, u32[]{:S(2)}, u32[]{:S(2)}) %collective-permute-start.1) | collective-permute-done | bytes 65568 | tf_op jit(solution)/shard_map/ppermute | solution.py:218
  18.9 0.9 fusion
  19.7 5.2 %collective-permute-start.4 = (bf16[16,2048]{1,0:T(8,128)(2,1)S(1)}, bf16[16,2048]{1,0:T(8,128)(2,1)S(1)}, u32[]{:S(2)}, u32[]{:S(2)}) collective-permute-start(bf16[16,2048]{1,0:T(8,128)(2,1)S(1)} %get-tuple-element.25), channel_id=1, source_target_pairs={{0,48},{16,64},{32,80},{48,96},{64,112},{80,0},{96,16},{112,32},{1... | collective-permute-start | bytes 196616 | tf_op jit(solution)/shard_map/ppermute | solution.py:218
  24.9 4.5 %collective-permute-done.4 = bf16[16,2048]{1,0:T(8,128)(2,1)S(1)} collective-permute-done((bf16[16,2048]{1,0:T(8,128)(2,1)S(1)}, bf16[16,2048]{1,0:T(8,128)(2,1)S(1)}, u32[]{:S(2)}, u32[]{:S(2)}) %collective-permute-start.4) | collective-permute-done | bytes 65568 | tf_op jit(solution)/shard_map/ppermute | solution.py:218
  29.4 3.7 %collective-permute-done.3 = bf16[16,2048]{1,0:T(8,128)(2,1)S(1)} collective-permute-done((bf16[16,2048]{1,0:T(8,128)(2,1)S(1)}, bf16[16,2048]{1,0:T(8,128)(2,1)S(1)}, u32[]{:S(2)}, u32[]{:S(2)}) %collective-permute-start.3) | collective-permute-done | bytes 65568 | tf_op jit(solution)/shard_map/ppermute | solution.py:218
  33.1 3.0 %collective-permute-start.5 = (bf16[16,2048]{1,0:T(8,128)(2,1)S(1)}, bf16[16,2048]{1,0:T(8,128)(2,1)S(1)}, u32[]{:S(2)}, u32[]{:S(2)}) collective-permute-start(bf16[16,2048]{1,0:T(8,128)(2,1)S(1)} %add_add_fusion), channel_id=1, source_target_pairs={{0,128},{16,144},{32,160},{48,176},{64,192},{80,208},{96,224},{112... | collective-permute-start | bytes 196616 | tf_op jit(solution)/shard_map/ppermute | solution.py:230
  36.1 2.9 %collective-permute-done.5 = bf16[16,2048]{1,0:T(8,128)(2,1)S(1)} collective-permute-done((bf16[16,2048]{1,0:T(8,128)(2,1)S(1)}, bf16[16,2048]{1,0:T(8,128)(2,1)S(1)}, u32[]{:S(2)}, u32[]{:S(2)}) %collective-permute-start.5) | collective-permute-done | bytes 65568 | tf_op jit(solution)/shard_map/ppermute | solution.py:230
  39.0 0.6 add.24.picked_ref
  39.6 1.7 %shard_map.79 = bf16[8,1216,128]{2,1,0:T(8,128)(2,1)} custom-call(bf16[8,1216,128]{2,1,0:T(8,128)(2,1)} %collective-permute-done.got_ref, bf16[16,2048]{1,0:T(8,128)(2,1)} %add.24.picked_ref), custom_call_target="tpu_custom_call", output_to_operand_aliasing={{}: (0, {})} | custom-call | bytes 524288 | tf_op jit(solution)/shard_map/pallas_call | solution.py:80
  41.3 0.0 copy-start.1
  41.3 0.0 copy-start
  41.4 34.6 %all_to_all.20.far_ref.pick_ref.prior_ref = bf16[8,1216,128]{2,1,0:T(8,128)(2,1)S(1)} all-to-all(bf16[8,1216,128]{2,1,0:T(8,128)(2,1)} %shard_map.79), channel_id=1, replica_groups={{0,2,4,6,8,10,12,14},{1,3,5,7,9,11,13,15},{16,18,20,22,24,26,28,30},{17..., dimensions={0} | all-to-all | bytes 4980736 | tf_op jit(solution)/shard_map/all_to_all | solution.py:255
  76.0 0.1 collective-permute-start.6
  76.1 1.9 %collective-permute-done.6.pick_ref = bf16[8,256,128]{2,1,0:T(8,128)(2,1)S(1)} collective-permute-done((bf16[8,256,128]{2,1,0:T(8,128)(2,1)S(1)}, bf16[8,256,128]{2,1,0:T(8,128)(2,1)S(1)}, u32[]{:S(2)}, u32[]{:S(2)}) %collective-permute-start.6) | collective-permute-done | bytes 524320 | tf_op jit(solution)/shard_map/ppermute | solution.py:230
  78.0 2.4 %shard_map.81 = (f32[8,16,2048]{2,1,0:T(8,128)S(1)}, bf16[8,16,768]{2,1,0:T(8,128)(2,1)S(1)}) custom-call(s32[1]{0:T(128)} %bitcast.1.me_ref, bf16[8,960,128]{2,1,0:T(8,128)(2,1)S(1)} %all-to-all-done.near_ref.prior_ref, bf16[8,1216,128]{2,1,0:T(8,128)(2,1)S(1)} %all_to_all.20.far_ref.pick_ref.prior_ref, ...), custom_call_target="tpu_custom_call" | custom-call | flops 805306368 | bytes 8126464 | tf_op jit(solution)/shard_map/pallas_call | solution.py:176
  80.4 0.2 collective-permute-start.7
  80.6 0.4 collective-permute-start.8
  81.0 2.4 %shard_map.80 = (f32[8,16,2048]{2,1,0:T(8,128)S(1)}, bf16[8,16,768]{2,1,0:T(8,128)(2,1)S(1)}) custom-call(s32[1]{0:T(128)} %bitcast.1.me_ref, bf16[8,960,128]{2,1,0:T(8,128)(2,1)S(1)} %all-to-all-done.near_ref.prior_ref, bf16[8,1216,128]{2,1,0:T(8,128)(2,1)S(1)} %all_to_all.20.far_ref.pick_ref.prior_ref, ...), custom_call_target="tpu_custom_call" | custom-call | flops 805306368 | bytes 8126464 | tf_op jit(solution)/shard_map/pallas_call | solution.py:176
  83.4 0.0 collective-permute-done.8.s_got
  83.4 0.1 shard_map.82
  83.5 18.0 %all_to_all.21.msg_ref = bf16[8,16,3584]{2,1,0:T(8,128)(2,1)} all-to-all(bf16[8,16,3584]{2,1,0:T(8,128)(2,1)S(1)} %shard_map.82), channel_id=1, replica_groups={{0,2,4,6,8,10,12,14},{1,3,5,7,9,11,13,15},{16,18,20,22,24,26,28,30},{17..., dimensions={0} | all-to-all | bytes 1835008 | tf_op jit(solution)/shard_map/all_to_all | solution.py:272
  101.6 1.8 %shard_map.84 = f32[16,16,128]{2,1,0:T(8,128)} custom-call(bf16[8,16,3584]{2,1,0:T(8,128)(2,1)} %all_to_all.21.msg_ref), custom_call_target="tpu_custom_call" | custom-call | flops 458752 | bytes 917504 | tf_op jit(solution)/shard_map/pallas_call | solution.py:273
  103.3 10.2 %all-to-all-start.3 = ((f32[16,16,128]{2,1,0:T(8,128)}), f32[16,16,128]{2,1,0:T(8,128)S(1)}, u32[]{:S(2)}, u32[]{:S(2)}) async-start(f32[16,16,128]{2,1,0:T(8,128)} %shard_map.84), calls=%async_computation.3 | async-start | bytes 262144 | tf_op jit(solution)/shard_map/all_to_all | solution.py:281
  113.5 2.4 %shard_map.83 = f32[16,12288]{1,0:T(8,128)} custom-call(s32[1]{0:T(128)} %bitcast.core_ref, bf16[8,16,3584]{2,1,0:T(8,128)(2,1)} %all_to_all.21.msg_ref, f32[16,12288]{1,0:T(8,128)} %bitcast.12), custom_call_target="tpu_custom_call" | custom-call | flops 196608 | bytes 1966080 | tf_op jit(solution)/shard_map/pallas_call | solution.py:283
  115.9 7.1 %all-to-all-done.3 = f32[16,16,128]{2,1,0:T(8,128)S(1)} async-done(((f32[16,16,128]{2,1,0:T(8,128)}), f32[16,16,128]{2,1,0:T(8,128)S(1)}, u32[]{:S(2)}, u32[]{:S(2)}) %all-to-all-start.3) | async-done | bytes 131104 | tf_op jit(solution)/shard_map/all_to_all | solution.py:281
  123.0 0.6 reduce_sum.9
  (9 shorter events, 0.1 us)
Async XLA Ops:
  4.2 35.4 %collective-permute-start = (bf16[8,1216,128]{2,1,0:T(8,128)(2,1)}, bf16[8,1216,128]{2,1,0:T(8,128)(2,1)}, u32[]{:S(2)}, u32[]{:S(2)}) collective-permute-start(bf16[8,1216,128]{2,1,0:T(8,128)(2,1)} %get-tuple-element.16), channel_id=1, source_target_pairs={{0,1},{1,0},{2,3},{3,2},{4,5},{5,4},{6,7},{7,6},{8,9},{9,8},{10,11... | collective-permute-start | bytes 7471112 | tf_op jit(solution)/shard_map/ppermute | solution.py:230
  4.2 37.2 %all-to-all-start = ((bf16[8,960,128]{2,1,0:T(8,128)(2,1)}), bf16[8,960,128]{2,1,0:T(8,128)(2,1)S(1)}, u32[]{:S(2)}, u32[]{:S(2)}) async-start(bf16[8,960,128]{2,1,0:T(8,128)(2,1)} %get-tuple-element.15), calls=%async_computation | async-start | bytes 3932160 | tf_op jit(solution)/shard_map/all_to_all | solution.py:249
  12.5 4.5 %collective-permute-start.2 = (bf16[16,2048]{1,0:T(8,128)(2,1)}, bf16[16,2048]{1,0:T(8,128)(2,1)S(1)}, u32[]{:S(2)}, u32[]{:S(2)}) collective-permute-start(bf16[16,2048]{1,0:T(8,128)(2,1)} %shard_map.78), channel_id=1, source_target_pairs={{0,16},{16,32},{32,48},{48,64},{64,80},{80,96},{96,112},{112,0},{1... | collective-permute-start | bytes 196616 | tf_op jit(solution)/shard_map/ppermute | solution.py:218
  14.4 4.5 %collective-permute-start.1 = (bf16[16,2048]{1,0:T(8,128)(2,1)}, bf16[16,2048]{1,0:T(8,128)(2,1)S(1)}, u32[]{:S(2)}, u32[]{:S(2)}) collective-permute-start(bf16[16,2048]{1,0:T(8,128)(2,1)} %shard_map.78), channel_id=1, source_target_pairs={{0,112},{16,0},{32,16},{48,32},{64,48},{80,64},{96,80},{112,96},{1... | collective-permute-start | bytes 196616 | tf_op jit(solution)/shard_map/ppermute | solution.py:218
  19.7 9.7 %collective-permute-start.4 = (bf16[16,2048]{1,0:T(8,128)(2,1)S(1)}, bf16[16,2048]{1,0:T(8,128)(2,1)S(1)}, u32[]{:S(2)}, u32[]{:S(2)}) collective-permute-start(bf16[16,2048]{1,0:T(8,128)(2,1)S(1)} %get-tuple-element.25), channel_id=1, source_target_pairs={{0,48},{16,64},{32,80},{48,96},{64,112},{80,0},{96,16},{112,32},{1... | collective-permute-start | bytes 196616 | tf_op jit(solution)/shard_map/ppermute | solution.py:218
  24.9 8.1 %collective-permute-start.3 = (bf16[16,2048]{1,0:T(8,128)(2,1)S(1)}, bf16[16,2048]{1,0:T(8,128)(2,1)S(1)}, u32[]{:S(2)}, u32[]{:S(2)}) collective-permute-start(bf16[16,2048]{1,0:T(8,128)(2,1)S(1)} %get-tuple-element.24), channel_id=1, source_target_pairs={{0,80},{16,96},{32,112},{48,0},{64,16},{80,32},{96,48},{112,64},{1... | collective-permute-start | bytes 196616 | tf_op jit(solution)/shard_map/ppermute | solution.py:218
  33.1 5.9 %collective-permute-start.5 = (bf16[16,2048]{1,0:T(8,128)(2,1)S(1)}, bf16[16,2048]{1,0:T(8,128)(2,1)S(1)}, u32[]{:S(2)}, u32[]{:S(2)}) collective-permute-start(bf16[16,2048]{1,0:T(8,128)(2,1)S(1)} %add_add_fusion), channel_id=1, source_target_pairs={{0,128},{16,144},{32,160},{48,176},{64,192},{80,208},{96,224},{112... | collective-permute-start | bytes 196616 | tf_op jit(solution)/shard_map/ppermute | solution.py:230
  41.3 36.7 %copy-start.1 = (f32[12288]{0:T(1024)S(1)}, f32[12288]{0:T(1024)}, u32[]{:S(2)}) copy-start(f32[12288]{0:T(1024)} %param.10) | copy-start | bytes 147460
  41.3 36.7 %copy-start = (bf16[2048,768]{1,0:T(8,128)(2,1)S(1)}, bf16[2048,768]{1,0:T(8,128)(2,1)}, u32[]{:S(2)}) copy-start(bf16[2048,768]{1,0:T(8,128)(2,1)} %proj_ref.3) | copy-start | bytes 9437188
  76.0 2.0 %collective-permute-start.6 = (bf16[8,256,128]{2,1,0:T(8,128)(2,1)S(1)}, bf16[8,256,128]{2,1,0:T(8,128)(2,1)S(1)}, u32[]{:S(2)}, u32[]{:S(2)}) collective-permute-start(bf16[8,256,128]{2,1,0:T(8,128)(2,1)S(1)} %slice.4), channel_id=1, source_target_pairs={{0,1},{1,0},{2,3},{3,2},{4,5},{5,4},{6,7},{7,6},{8,9},{9,8},{10,11... | collective-permute-start | bytes 1572872 | tf_op jit(solution)/shard_map/ppermute | solution.py:230
  80.4 3.0 %collective-permute-start.7 = (f32[8,16,2048]{2,1,0:T(8,128)S(1)}, f32[8,16,2048]{2,1,0:T(8,128)S(1)}, u32[]{:S(2)}, u32[]{:S(2)}) collective-permute-start(f32[8,16,2048]{2,1,0:T(8,128)S(1)} %get-tuple-element.21), channel_id=1, source_target_pairs={{0,1},{1,0},{2,3},{3,2},{4,5},{5,4},{6,7},{7,6},{8,9},{9,8},{10,11... | collective-permute-start | bytes 3145736 | tf_op jit(solution)/shard_map/ppermute | solution.py:230
  80.6 2.8 %collective-permute-start.8 = (bf16[8,16,768]{2,1,0:T(8,128)(2,1)S(1)}, bf16[8,16,768]{2,1,0:T(8,128)(2,1)S(1)}, u32[]{:S(2)}, u32[]{:S(2)}) collective-permute-start(bf16[8,16,768]{2,1,0:T(8,128)(2,1)S(1)} %get-tuple-element.23), channel_id=1, source_target_pairs={{0,1},{1,0},{2,3},{3,2},{4,5},{5,4},{6,7},{7,6},{8,9},{9,8},{10,11... | collective-permute-start | bytes 589832 | tf_op jit(solution)/shard_map/ppermute | solution.py:230
  103.3 19.6 %all-to-all-start.3 = ((f32[16,16,128]{2,1,0:T(8,128)}), f32[16,16,128]{2,1,0:T(8,128)S(1)}, u32[]{:S(2)}, u32[]{:S(2)}) async-start(f32[16,16,128]{2,1,0:T(8,128)} %shard_map.84), calls=%async_computation.3 | async-start | bytes 262144 | tf_op jit(solution)/shard_map/all_to_all | solution.py:281

commit v7 on v5

--- a/solution.py
+++ b/solution.py
@@ -173,7 +173,7 @@
         cols = slice(n * WIDE, (n + 1) * WIDE)
         part = lax.dot_general(weighted[...], proj_ref[cols], NT, preferred_element_type=F32)
         p_own[:, :, cols] = part[:half].reshape(chips, evo, WIDE)
-        p_other[:, :, cols] = part[half:].reshape(chips, evo, WIDE)
+        p_other[:, :, cols] = part[half:].astype(BF16).reshape(chips, evo, WIDE)
 
 
 def main_step(me, near, far, other, apod, proj, evo, count):
@@ -184,7 +184,7 @@
         main_kernel,
         out_shape=(
             jax.ShapeDtypeStruct((chips, evo, prows), F32),
-            jax.ShapeDtypeStruct((chips, evo, prows), F32),
+            jax.ShapeDtypeStruct((chips, evo, prows), BF16),
             jax.ShapeDtypeStruct((chips, evo, sub), BF16),
             jax.ShapeDtypeStruct((chips, evo, sub), BF16),
         ),
@@ -198,7 +198,7 @@
 
 def home_kernel(p_own, p_got, s_own, s_got, out_ref):
     prows, sub = p_own.shape[2], s_own.shape[2]
-    out_ref[:, :, :prows] = (p_own[...] + p_got[...]).astype(BF16)
+    out_ref[:, :, :prows] = (p_own[...] + p_got[...].astype(F32)).astype(BF16)
     out_ref[:, :, prows : prows + sub] = s_own[...]
     out_ref[:, :, prows + sub :] = s_got[...]
 

time: 124 us -> 123 us (level)
  no operation moved by 1% of the time
where the time goes in v7:
time: 123 us
  blocking collectives  52.6 us (43%)
  starting transfers between devices  26.4 us (21%)
  waiting for transfers between devices  26.1 us (21%)
  Pallas kernels  14.7 us (12%)
  other arithmetic  2.13 us (2%)
    all_to_all x1, blocking collectives, on_device(): far_rows = to_chips(joined)  34.6 us
    all_to_all x1, blocking collectives, on_device(): home = to_chips(home)  18 us
    ppermute x4, waiting for transfers between devices, turn(): lax.ppermute(y, 'row', [(h * ring + z, h * ring + (z + by) % ring) for h...  12.5 us
    all_to_all x1, starting transfers between devices, on_device(): share = lax.all_to_all(share, 'row', 0, 0, tiled=True)  10.2 us
    ppermute x4, starting transfers between devices, turn(): lax.ppermute(y, 'row', [(h * ring + z, h * ring + (z + by) % ring) for h...  7.24 us
    all_to_all x1, waiting for transfers between devices, on_device(): share = lax.all_to_all(share, 'row', 0, 0, tiled=True)  7.1 us
    ppermute x5, waiting for transfers between devices, swap(): return lax.ppermute(x, axis, [(i, i ^ bits) for i in range(n)])  6.45 us
    all_to_all x1, starting transfers between devices, on_device(): near_rows = to_chips(keep)  5.31 us
  transfers between devices with their start and end apart: 11, of which 8 were waited for; matrix products, arithmetic and copies ran while one was open for 1% of the time, Pallas kernels for 6%

profile of v7, /device:TPU:32, one launch (start us, length us, event | category | flops | bytes accessed | tf_op | source)
XLA Modules:
  0.0 122.6 jit_solution(1141110008562664805)
XLA Ops:
  0.6 3.5 %shard_map.77 = (bf16[8,960,128]{2,1,0:T(8,128)(2,1)}, bf16[8,1216,128]{2,1,0:T(8,128)(2,1)}) custom-call(s32[1]{0:T(128)} %bitcast.core_ref, bf16[12288,128]{1,0:T(8,128)(2,1)} %obs_ref.1, f32[16,12288]{1,0:T(8,128)} %bitcast.10), custom_call_target="tpu_custom_call" | custom-call | bytes 7864320 | tf_op jit(solution)/shard_map/pallas_call | solution.py:47
  4.1 0.0 collective-permute-start
  4.1 5.3 %all-to-all-start = ((bf16[8,960,128]{2,1,0:T(8,128)(2,1)}), bf16[8,960,128]{2,1,0:T(8,128)(2,1)S(1)}, u32[]{:S(2)}, u32[]{:S(2)}) async-start(bf16[8,960,128]{2,1,0:T(8,128)(2,1)} %get-tuple-element.15), calls=%async_computation | async-start | bytes 3932160 | tf_op jit(solution)/shard_map/all_to_all | solution.py:258
  9.5 3.0 %shard_map.78 = bf16[16,2048]{1,0:T(8,128)(2,1)} custom-call(s32[1]{0:T(128)} %bitcast.3.first_ref, s32[1,2048]{1,0:T(1,128)} %bitcast.15, bf16[16,12288]{1,0:T(8,128)(2,1)} %bitcast.14), custom_call_target="tpu_custom_call" | custom-call | flops 805306368 | bytes 458752 | tf_op jit(solution)/shard_map/pallas_call | solution.py:114
  12.4 1.9 %collective-permute-start.2 = (bf16[16,2048]{1,0:T(8,128)(2,1)}, bf16[16,2048]{1,0:T(8,128)(2,1)S(1)}, u32[]{:S(2)}, u32[]{:S(2)}) collective-permute-start(bf16[16,2048]{1,0:T(8,128)(2,1)} %shard_map.78), channel_id=1, source_target_pairs={{0,16},{16,32},{32,48},{48,64},{64,80},{80,96},{96,112},{112,0},{1... | collective-permute-start | bytes 196616 | tf_op jit(solution)/shard_map/ppermute | solution.py:227
  14.4 0.1 collective-permute-start.1
  14.5 2.4 %collective-permute-done.2 = bf16[16,2048]{1,0:T(8,128)(2,1)S(1)} collective-permute-done((bf16[16,2048]{1,0:T(8,128)(2,1)}, bf16[16,2048]{1,0:T(8,128)(2,1)S(1)}, u32[]{:S(2)}, u32[]{:S(2)}) %collective-permute-start.2) | collective-permute-done | bytes 65568 | tf_op jit(solution)/shard_map/ppermute | solution.py:227
  16.9 1.9 %collective-permute-done.1 = bf16[16,2048]{1,0:T(8,128)(2,1)S(1)} collective-permute-done((bf16[16,2048]{1,0:T(8,128)(2,1)}, bf16[16,2048]{1,0:T(8,128)(2,1)S(1)}, u32[]{:S(2)}, u32[]{:S(2)}) %collective-permute-start.1) | collective-permute-done | bytes 65568 | tf_op jit(solution)/shard_map/ppermute | solution.py:227
  18.8 0.9 fusion
  19.7 5.2 %collective-permute-start.4 = (bf16[16,2048]{1,0:T(8,128)(2,1)S(1)}, bf16[16,2048]{1,0:T(8,128)(2,1)S(1)}, u32[]{:S(2)}, u32[]{:S(2)}) collective-permute-start(bf16[16,2048]{1,0:T(8,128)(2,1)S(1)} %get-tuple-element.25), channel_id=1, source_target_pairs={{0,48},{16,64},{32,80},{48,96},{64,112},{80,0},{96,16},{112,32},{1... | collective-permute-start | bytes 196616 | tf_op jit(solution)/shard_map/ppermute | solution.py:227
  24.9 4.5 %collective-permute-done.4 = bf16[16,2048]{1,0:T(8,128)(2,1)S(1)} collective-permute-done((bf16[16,2048]{1,0:T(8,128)(2,1)S(1)}, bf16[16,2048]{1,0:T(8,128)(2,1)S(1)}, u32[]{:S(2)}, u32[]{:S(2)}) %collective-permute-start.4) | collective-permute-done | bytes 65568 | tf_op jit(solution)/shard_map/ppermute | solution.py:227
  29.4 3.7 %collective-permute-done.3 = bf16[16,2048]{1,0:T(8,128)(2,1)S(1)} collective-permute-done((bf16[16,2048]{1,0:T(8,128)(2,1)S(1)}, bf16[16,2048]{1,0:T(8,128)(2,1)S(1)}, u32[]{:S(2)}, u32[]{:S(2)}) %collective-permute-start.3) | collective-permute-done | bytes 65568 | tf_op jit(solution)/shard_map/ppermute | solution.py:227
  33.1 3.0 %collective-permute-start.5 = (bf16[16,2048]{1,0:T(8,128)(2,1)S(1)}, bf16[16,2048]{1,0:T(8,128)(2,1)S(1)}, u32[]{:S(2)}, u32[]{:S(2)}) collective-permute-start(bf16[16,2048]{1,0:T(8,128)(2,1)S(1)} %add_add_fusion), channel_id=1, source_target_pairs={{0,128},{16,144},{32,160},{48,176},{64,192},{80,208},{96,224},{112... | collective-permute-start | bytes 196616 | tf_op jit(solution)/shard_map/ppermute | solution.py:239
  36.0 2.9 %collective-permute-done.5 = bf16[16,2048]{1,0:T(8,128)(2,1)S(1)} collective-permute-done((bf16[16,2048]{1,0:T(8,128)(2,1)S(1)}, bf16[16,2048]{1,0:T(8,128)(2,1)S(1)}, u32[]{:S(2)}, u32[]{:S(2)}) %collective-permute-start.5) | collective-permute-done | bytes 65568 | tf_op jit(solution)/shard_map/ppermute | solution.py:239
  38.9 0.6 add.24.picked_ref
  39.6 1.7 %shard_map.79 = bf16[8,1216,128]{2,1,0:T(8,128)(2,1)} custom-call(bf16[8,1216,128]{2,1,0:T(8,128)(2,1)} %collective-permute-done.got_ref, bf16[16,2048]{1,0:T(8,128)(2,1)} %add.24.picked_ref), custom_call_target="tpu_custom_call", output_to_operand_aliasing={{}: (0, {})} | custom-call | bytes 524288 | tf_op jit(solution)/shard_map/pallas_call | solution.py:80
  41.3 0.0 copy-start.1
  41.3 0.0 copy-start
  41.3 34.6 %all_to_all.20.far_ref = bf16[8,1216,128]{2,1,0:T(8,128)(2,1)S(1)} all-to-all(bf16[8,1216,128]{2,1,0:T(8,128)(2,1)} %shard_map.79), channel_id=1, replica_groups={{0,2,4,6,8,10,12,14},{1,3,5,7,9,11,13,15},{16,18,20,22,24,26,28,30},{17..., dimensions={0} | all-to-all | bytes 4980736 | tf_op jit(solution)/shard_map/all_to_all | solution.py:264
  76.0 0.1 collective-permute-start.6
  76.1 1.9 %collective-permute-done.6.other_ref = bf16[8,256,128]{2,1,0:T(8,128)(2,1)S(1)} collective-permute-done((bf16[8,256,128]{2,1,0:T(8,128)(2,1)S(1)}, bf16[8,256,128]{2,1,0:T(8,128)(2,1)S(1)}, u32[]{:S(2)}, u32[]{:S(2)}) %collective-permute-start.6) | collective-permute-done | bytes 524320 | tf_op jit(solution)/shard_map/ppermute | solution.py:239
  78.0 2.2 %shard_map.80 = (f32[8,16,2048]{2,1,0:T(8,128)S(1)}, bf16[8,16,2048]{2,1,0:T(8,128)(2,1)S(1)}, bf16[8,16,768]{2,1,0:T(8,128)(2,1)S(1)}, bf16[8,16,768]{2,1,0:T(8,128)(2,1)S(1)}) custom-call(s32[1]{0:T(128)} %bitcast.1.me_ref, bf16[8,960,128]{2,1,0:T(8,128)(2,1)S(1)} %all-to-all-done.near_ref, bf16[8,1216,128]{2,1,0:T(8,128)(2,1)S(1)} %all_to_all.20.far_ref, ...), custom_call_target="tpu_custom_call" | custom-call | flops 1610612736 | bytes 9175040 | tf_op jit(solution)/shard_map/pallas_call | solution.py:183
  80.2 0.2 collective-permute-start.7
  80.4 0.4 collective-permute-start.8
  80.8 1.7 %collective-permute-done.8.s_got = bf16[8,16,768]{2,1,0:T(8,128)(2,1)S(1)} collective-permute-done((bf16[8,16,768]{2,1,0:T(8,128)(2,1)S(1)}, bf16[8,16,768]{2,1,0:T(8,128)(2,1)S(1)}, u32[]{:S(2)}, u32[]{:S(2)}) %collective-permute-start.8) | collective-permute-done | bytes 196640 | tf_op jit(solution)/shard_map/ppermute | solution.py:239
  82.5 0.1 shard_map.81
  82.6 18.0 %all_to_all.21.msg_ref = bf16[8,16,3584]{2,1,0:T(8,128)(2,1)} all-to-all(bf16[8,16,3584]{2,1,0:T(8,128)(2,1)S(1)} %shard_map.81), channel_id=1, replica_groups={{0,2,4,6,8,10,12,14},{1,3,5,7,9,11,13,15},{16,18,20,22,24,26,28,30},{17..., dimensions={0} | all-to-all | bytes 1835008 | tf_op jit(solution)/shard_map/all_to_all | solution.py:280
  100.6 1.8 %shard_map.83 = f32[16,16,128]{2,1,0:T(8,128)} custom-call(bf16[8,16,3584]{2,1,0:T(8,128)(2,1)} %all_to_all.21.msg_ref), custom_call_target="tpu_custom_call" | custom-call | flops 458752 | bytes 917504 | tf_op jit(solution)/shard_map/pallas_call | solution.py:281
  102.3 10.2 %all-to-all-start.3 = ((f32[16,16,128]{2,1,0:T(8,128)}), f32[16,16,128]{2,1,0:T(8,128)S(1)}, u32[]{:S(2)}, u32[]{:S(2)}) async-start(f32[16,16,128]{2,1,0:T(8,128)} %shard_map.83), calls=%async_computation.3 | async-start | bytes 262144 | tf_op jit(solution)/shard_map/all_to_all | solution.py:289
  112.5 2.4 %shard_map.82 = f32[16,12288]{1,0:T(8,128)} custom-call(s32[1]{0:T(128)} %bitcast.core_ref, bf16[8,16,3584]{2,1,0:T(8,128)(2,1)} %all_to_all.21.msg_ref, f32[16,12288]{1,0:T(8,128)} %bitcast.11), custom_call_target="tpu_custom_call" | custom-call | flops 196608 | bytes 1966080 | tf_op jit(solution)/shard_map/pallas_call | solution.py:291
  114.9 7.1 %all-to-all-done.3 = f32[16,16,128]{2,1,0:T(8,128)S(1)} async-done(((f32[16,16,128]{2,1,0:T(8,128)}), f32[16,16,128]{2,1,0:T(8,128)S(1)}, u32[]{:S(2)}, u32[]{:S(2)}) %all-to-all-start.3) | async-done | bytes 131104 | tf_op jit(solution)/shard_map/all_to_all | solution.py:289
  122.0 0.6 reduce_sum.9
  (8 shorter events, 0.1 us)
Async XLA Ops:
  4.1 35.4 %collective-permute-start = (bf16[8,1216,128]{2,1,0:T(8,128)(2,1)}, bf16[8,1216,128]{2,1,0:T(8,128)(2,1)}, u32[]{:S(2)}, u32[]{:S(2)}) collective-permute-start(bf16[8,1216,128]{2,1,0:T(8,128)(2,1)} %get-tuple-element.16), channel_id=1, source_target_pairs={{0,1},{1,0},{2,3},{3,2},{4,5},{5,4},{6,7},{7,6},{8,9},{9,8},{10,11... | collective-permute-start | bytes 7471112 | tf_op jit(solution)/shard_map/ppermute | solution.py:239
  4.1 37.2 %all-to-all-start = ((bf16[8,960,128]{2,1,0:T(8,128)(2,1)}), bf16[8,960,128]{2,1,0:T(8,128)(2,1)S(1)}, u32[]{:S(2)}, u32[]{:S(2)}) async-start(bf16[8,960,128]{2,1,0:T(8,128)(2,1)} %get-tuple-element.15), calls=%async_computation | async-start | bytes 3932160 | tf_op jit(solution)/shard_map/all_to_all | solution.py:258
  12.4 4.5 %collective-permute-start.2 = (bf16[16,2048]{1,0:T(8,128)(2,1)}, bf16[16,2048]{1,0:T(8,128)(2,1)S(1)}, u32[]{:S(2)}, u32[]{:S(2)}) collective-permute-start(bf16[16,2048]{1,0:T(8,128)(2,1)} %shard_map.78), channel_id=1, source_target_pairs={{0,16},{16,32},{32,48},{48,64},{64,80},{80,96},{96,112},{112,0},{1... | collective-permute-start | bytes 196616 | tf_op jit(solution)/shard_map/ppermute | solution.py:227
  14.4 4.5 %collective-permute-start.1 = (bf16[16,2048]{1,0:T(8,128)(2,1)}, bf16[16,2048]{1,0:T(8,128)(2,1)S(1)}, u32[]{:S(2)}, u32[]{:S(2)}) collective-permute-start(bf16[16,2048]{1,0:T(8,128)(2,1)} %shard_map.78), channel_id=1, source_target_pairs={{0,112},{16,0},{32,16},{48,32},{64,48},{80,64},{96,80},{112,96},{1... | collective-permute-start | bytes 196616 | tf_op jit(solution)/shard_map/ppermute | solution.py:227
  19.7 9.7 %collective-permute-start.4 = (bf16[16,2048]{1,0:T(8,128)(2,1)S(1)}, bf16[16,2048]{1,0:T(8,128)(2,1)S(1)}, u32[]{:S(2)}, u32[]{:S(2)}) collective-permute-start(bf16[16,2048]{1,0:T(8,128)(2,1)S(1)} %get-tuple-element.25), channel_id=1, source_target_pairs={{0,48},{16,64},{32,80},{48,96},{64,112},{80,0},{96,16},{112,32},{1... | collective-permute-start | bytes 196616 | tf_op jit(solution)/shard_map/ppermute | solution.py:227
  24.9 8.1 %collective-permute-start.3 = (bf16[16,2048]{1,0:T(8,128)(2,1)S(1)}, bf16[16,2048]{1,0:T(8,128)(2,1)S(1)}, u32[]{:S(2)}, u32[]{:S(2)}) collective-permute-start(bf16[16,2048]{1,0:T(8,128)(2,1)S(1)} %get-tuple-element.24), channel_id=1, source_target_pairs={{0,80},{16,96},{32,112},{48,0},{64,16},{80,32},{96,48},{112,64},{1... | collective-permute-start | bytes 196616 | tf_op jit(solution)/shard_map/ppermute | solution.py:227
  33.1 5.9 %collective-permute-start.5 = (bf16[16,2048]{1,0:T(8,128)(2,1)S(1)}, bf16[16,2048]{1,0:T(8,128)(2,1)S(1)}, u32[]{:S(2)}, u32[]{:S(2)}) collective-permute-start(bf16[16,2048]{1,0:T(8,128)(2,1)S(1)} %add_add_fusion), channel_id=1, source_target_pairs={{0,128},{16,144},{32,160},{48,176},{64,192},{80,208},{96,224},{112... | collective-permute-start | bytes 196616 | tf_op jit(solution)/shard_map/ppermute | solution.py:239
  41.3 36.7 %copy-start.1 = (f32[12288]{0:T(1024)S(1)}, f32[12288]{0:T(1024)}, u32[]{:S(2)}) copy-start(f32[12288]{0:T(1024)} %param.10) | copy-start | bytes 147460
  41.3 36.7 %copy-start = (bf16[2048,768]{1,0:T(8,128)(2,1)S(1)}, bf16[2048,768]{1,0:T(8,128)(2,1)}, u32[]{:S(2)}) copy-start(bf16[2048,768]{1,0:T(8,128)(2,1)} %proj_ref.1) | copy-start | bytes 9437188
  76.0 2.0 %collective-permute-start.6 = (bf16[8,256,128]{2,1,0:T(8,128)(2,1)S(1)}, bf16[8,256,128]{2,1,0:T(8,128)(2,1)S(1)}, u32[]{:S(2)}, u32[]{:S(2)}) collective-permute-start(bf16[8,256,128]{2,1,0:T(8,128)(2,1)S(1)} %slice.4), channel_id=1, source_target_pairs={{0,1},{1,0},{2,3},{3,2},{4,5},{5,4},{6,7},{7,6},{8,9},{9,8},{10,11... | collective-permute-start | bytes 1572872 | tf_op jit(solution)/shard_map/ppermute | solution.py:239
  80.2 2.3 %collective-permute-start.7 = (bf16[8,16,2048]{2,1,0:T(8,128)(2,1)S(1)}, bf16[8,16,2048]{2,1,0:T(8,128)(2,1)S(1)}, u32[]{:S(2)}, u32[]{:S(2)}) collective-permute-start(bf16[8,16,2048]{2,1,0:T(8,128)(2,1)S(1)} %get-tuple-element.21), channel_id=1, source_target_pairs={{0,1},{1,0},{2,3},{3,2},{4,5},{5,4},{6,7},{7,6},{8,9},{9,8},{10,11... | collective-permute-start | bytes 1572872 | tf_op jit(solution)/shard_map/ppermute | solution.py:239
  80.4 2.1 %collective-permute-start.8 = (bf16[8,16,768]{2,1,0:T(8,128)(2,1)S(1)}, bf16[8,16,768]{2,1,0:T(8,128)(2,1)S(1)}, u32[]{:S(2)}, u32[]{:S(2)}) collective-permute-start(bf16[8,16,768]{2,1,0:T(8,128)(2,1)S(1)} %get-tuple-element.23), channel_id=1, source_target_pairs={{0,1},{1,0},{2,3},{3,2},{4,5},{5,4},{6,7},{7,6},{8,9},{9,8},{10,11... | collective-permute-start | bytes 589832 | tf_op jit(solution)/shard_map/ppermute | solution.py:239
  102.3 19.6 %all-to-all-start.3 = ((f32[16,16,128]{2,1,0:T(8,128)}), f32[16,16,128]{2,1,0:T(8,128)S(1)}, u32[]{:S(2)}, u32[]{:S(2)}) async-start(f32[16,16,128]{2,1,0:T(8,128)} %shard_map.83), calls=%async_computation.3 | async-start | bytes 262144 | tf_op jit(solution)/shard_map/all_to_all | solution.py:289
